TPU v7x, 128 devices: a whole 4x4x4 slice. The times are simulated.
128 devices in a mesh: section: 8 (over x, core), expert: 16 (over y, z).
Axes of the slice: x: 4, y: 4, z: 4, core: 2. Of those that a mesh axis runs over, the one named last changes fastest.
Arguments:
- act_in: bfloat16 [8, 2048, 6144], P('section', 'expert'), may hold values from -6 to 6
- saved_in: bfloat16 [8, 2048, 6144], P('section', 'expert'), may hold values from -6 to 6
- grad_in: bfloat16 [8, 2048, 6144], P('section', 'expert'), may hold values from -6 to 6
- fwd_routes: int32 [8, 2048, 2], P('section', 'expert'), may hold values from 0 to 7, as said below
- bwd_routes: int32 [8, 2048, 2], P('section', 'expert'), may hold values from 0 to 7, as said below
- w_gate: bfloat16 [8, 6144, 8192], P('section', None, 'expert'), may hold values from -0.078125 to 0.078125
- w_up: bfloat16 [8, 6144, 8192], P('section', None, 'expert'), may hold values from -0.078125 to 0.078125
- w_down: bfloat16 [8, 8192, 6144], P('section', 'expert'), may hold values from -0.0625 to 0.0625
- router: float32 [8, 6144, 8], P('section'), may hold values from -0.078125 to 0.078125
- norm_gain: float32 [8, 6144], P('section'), may hold values from 0.1 to 1.9
Outputs:
- act_out: bfloat16 [8, 2048, 6144], P('section', 'expert')
- grad_out: bfloat16 [8, 2048, 6144], P('section', 'expert')
Inputs may be any that keep to these rules, and one draw needn't show every extreme that they name: `fwd_routes`: per section, the 128 rows of one device name expert 0 between 16 and 32 times, and in every section some device's rows name it exactly 32 times; a token's two experts differ. `bwd_routes`: per section, the 128 rows of one device name expert 0 between 16 and 32 times, and in every section some device's rows name it exactly 32 times; a token's two experts differ.
All inputs are finite; a program needn't handle non-finite values.
Results may differ from a plain program's by a relative error of at most 0.007.
Values may be sent and summed in bfloat16 or wider, within the bound.
A program may use at most 128 MiB of HBM per device.

v0:
```python
import jax
import jax.numpy as jnp
from jax import lax
from jax.sharding import PartitionSpec as P

epsilon = 1e-05
highest = lax.Precision.HIGHEST


def shifted(value, axis, steps):
    count = lax.axis_size(axis)
    pairs = [(source, (source + steps) % count) for source in range(count)]
    return lax.ppermute(value, axis, pairs)


def norm_route(inputs, gain_row, router_mat, chosen_ids):
    inverse = lax.rsqrt(jnp.mean(inputs * inputs, axis=1, keepdims=True) + epsilon)
    normed = inputs * inverse * gain_row[None, :]
    logits = jnp.dot(normed, router_mat, precision=highest)
    onehot = (
        chosen_ids[:, :, None] == jnp.arange(router_mat.shape[1], dtype=jnp.int32)[None, None, :]
    ).astype(jnp.float32)
    picked = jnp.sum(onehot * logits[:, None, :], axis=2)
    first_share = jax.nn.sigmoid(picked[:, 0] - picked[:, 1])
    shares = jnp.stack([first_share, 1.0 - first_share], axis=1)
    window_weight = jnp.sum(shares * (chosen_ids == 0).astype(jnp.float32), axis=1)
    return (normed, window_weight)


def assign_window(chosen_ids, capacity):
    named_zero = jnp.sum((chosen_ids == 0).astype(jnp.int32), axis=1)
    rank_in = jnp.cumsum(named_zero) - named_zero
    slot_of = jnp.where(named_zero > 0, rank_in, capacity)
    matches = (slot_of[None, :] == jnp.arange(capacity, dtype=jnp.int32)[:, None]).astype(jnp.int32)
    token_ids = jnp.arange(chosen_ids.shape[0], dtype=jnp.int32) + 1
    source = jnp.sum(matches * token_ids[None, :], axis=1) - 1
    return (slot_of, source)


def fill_rows(values, source):
    picked = jnp.take(values, jnp.maximum(source, 0), axis=0)
    keep = (source >= 0).reshape((-1,) + (1,) * (values.ndim - 1))
    return jnp.where(keep, picked, jnp.zeros_like(picked))


def unfill(lookup, slot_of):
    padded = jnp.concatenate([lookup, jnp.zeros((1,) + lookup.shape[1:], lookup.dtype)], axis=0)
    return jnp.take(padded, slot_of, axis=0)


def forward_part(slot_rows, gate_cols, up_cols, down_rows):
    gate_pre = jnp.dot(slot_rows, gate_cols, preferred_element_type=jnp.float32)
    up_pre = jnp.dot(slot_rows, up_cols, preferred_element_type=jnp.float32)
    active = (gate_pre * jax.nn.sigmoid(gate_pre) * up_pre).astype(jnp.bfloat16)
    return jnp.dot(active, down_rows, preferred_element_type=jnp.float32).astype(jnp.bfloat16)


def backward_part(slot_rows, upstream_rows, weight_col, gate_cols, up_cols, down_rows):
    last_dims = (((1,), (1,)), ((), ()))
    gate_pre = jnp.dot(slot_rows, gate_cols, preferred_element_type=jnp.float32)
    up_pre = jnp.dot(slot_rows, up_cols, preferred_element_type=jnp.float32)
    gate_sig = jax.nn.sigmoid(gate_pre)
    silu_val = gate_pre * gate_sig
    active = (silu_val * up_pre).astype(jnp.bfloat16)
    back_cols = lax.dot_general(
        upstream_rows, down_rows, last_dims, preferred_element_type=jnp.float32
    )
    slope_part = jnp.sum(active.astype(jnp.float32) * back_cols, axis=1).astype(jnp.bfloat16)
    act_cot = weight_col[:, None] * back_cols
    gate_cot = (act_cot * up_pre * gate_sig * (1.0 + gate_pre * (1.0 - gate_sig))).astype(
        jnp.bfloat16
    )
    up_cot = (act_cot * silu_val).astype(jnp.bfloat16)
    row_part = (
        lax.dot_general(gate_cot, gate_cols, last_dims, preferred_element_type=jnp.float32)
        + lax.dot_general(up_cot, up_cols, last_dims, preferred_element_type=jnp.float32)
    ).astype(jnp.bfloat16)
    return (row_part, slope_part)


def run_forward(slot_rows, weights_three):
    return forward_part(slot_rows, weights_three[0], weights_three[1], weights_three[2])


def run_backward(slot_rows, upstream_rows, weight_col, weights_three):
    return backward_part(
        slot_rows, upstream_rows, weight_col, weights_three[0], weights_three[1], weights_three[2]
    )


def local(
    act_in, saved_in, grad_in, fwd_routes, bwd_routes, w_gate, w_up, w_down, router, norm_gain
):
    tok_rows = act_in.shape[1]
    capacity = tok_rows // 4
    weights_three = (w_gate[0], w_up[0], w_down[0])
    gain_row = norm_gain[0]
    router_mat = router[0]
    fwd_x = act_in[0].astype(jnp.float32)
    fwd_ids = fwd_routes[0]
    normed_f, weight_f = norm_route(fwd_x, gain_row, router_mat, fwd_ids)
    slot_f, source_f = assign_window(fwd_ids, capacity)
    send_f = fill_rows(normed_f.astype(jnp.bfloat16), source_f)
    back_x = saved_in[0].astype(jnp.float32)
    upstream = grad_in[0]
    bwd_ids = bwd_routes[0]

    def front(inputs):
        return norm_route(inputs, gain_row, router_mat, bwd_ids)

    (normed_b, weight_b), pullback = jax.vjp(front, back_x)
    slot_b, source_b = assign_window(bwd_ids, capacity)
    send_h = fill_rows(normed_b.astype(jnp.bfloat16), source_b)
    send_u = fill_rows(upstream, source_b)
    send_q = fill_rows(weight_b.astype(jnp.bfloat16), source_b)
    gathered_f = lax.all_gather(send_f, "expert", axis=0, tiled=True)
    out_part = run_forward(gathered_f, weights_three)
    expert_out = lax.psum_scatter(
        out_part.astype(jnp.float32).astype(jnp.bfloat16), "expert", scatter_dimension=0, tiled=True
    ).astype(jnp.float32)
    gathered_b = (
        lax.all_gather(send_h, "expert", axis=0, tiled=True),
        lax.all_gather(send_u, "expert", axis=0, tiled=True),
        lax.all_gather(send_q, "expert", axis=0, tiled=True),
    )
    row_part, slope_part = run_backward(
        gathered_b[0], gathered_b[1], gathered_b[2].astype(jnp.float32), weights_three
    )
    row_cot, slope_sum = (
        lax.psum_scatter(
            row_part.astype(jnp.float32).astype(jnp.bfloat16),
            "expert",
            scatter_dimension=0,
            tiled=True,
        ).astype(jnp.float32),
        lax.psum_scatter(
            slope_part.astype(jnp.float32).astype(jnp.bfloat16),
            "expert",
            scatter_dimension=0,
            tiled=True,
        ).astype(jnp.float32),
    )
    picked_f = unfill(expert_out, slot_f)
    layer_out = (fwd_x + weight_f[:, None] * picked_f).astype(jnp.bfloat16)
    act_out = shifted(layer_out[None], "section", 1)
    cot_normed = unfill(row_cot, slot_b)
    cot_weight = unfill(slope_sum, slot_b)
    d_rows = pullback((cot_normed, cot_weight))[0]
    grad_rows = (upstream.astype(jnp.float32) + d_rows).astype(jnp.bfloat16)
    grad_out = shifted(grad_rows[None], "section", -1)
    return (act_out, grad_out)


def solution(mesh):
    in_specs = (
        P("section", "expert", None),
        P("section", "expert", None),
        P("section", "expert", None),
        P("section", "expert", None),
        P("section", "expert", None),
        P("section", None, "expert"),
        P("section", None, "expert"),
        P("section", "expert", None),
        P("section", None, None),
        P("section", None),
    )
    out_specs = (P("section", "expert", None), P("section", "expert", None))
    return jax.shard_map(local, mesh=mesh, in_specs=in_specs, out_specs=out_specs, check_vma=False)
```

profile of v0, /device:TPU:1, one launch (start us, length us, event | category | flops | bytes accessed | tf_op | source)
XLA Modules:
  0.0 419.4 jit_solution(15917102283844666207)
XLA Ops:
  9.7 1.9 fusion.30
  12.1 2.1 fusion.24
  14.1 1.5 gather_fusion.2
  15.7 2.0 select_select_fusion.2
  17.7 3.5 gather_fusion.5
  21.3 1.5 gather_fusion.4
  22.8 2.2 select_select_fusion
  25.8 56.4 %all-gather.4.cloned.1.call-done = bf16[512,6144]{1,0:T(8,128)(2,1)} async-done(((bf16[32,6144]{1,0:T(8,128)(2,1)}), bf16[512,6144]{1,0:T(8,128)(2,1)}) %all-gather.4.cloned.1.call-update) | async-done | bytes 6291472 | tf_op jit(solution)/shard_map/all_gather | solution.py:116
  82.3 8.2 %fusion.13 = f32[512,512]{1,0:T(8,128)S(1)} fusion(bf16[512,6144]{1,0:T(8,128)(2,1)} %all-gather.4.cloned.1.call-done, bf16[1,6144,512]{2,1,0:T(8,128)(2,1)} %param.19), kind=kOutput, calls=%fused_computation.23 | convolution fusion | flops 3221225472 | bytes 13631488 | tf_op jit(solution)/shard_map/dot_general | solution.py:52
  90.5 6.4 %fusion.49 = bf16[512,512]{1,0:T(8,128)(2,1)S(1)} fusion(bf16[512,6144]{1,0:T(8,128)(2,1)S(1)} %copy-done.11, bf16[1,6144,512]{2,1,0:T(8,128)(2,1)} %param.20, f32[512,512]{1,0:T(8,128)S(1)} %fusion.13), kind=kOutput, calls=%fused_computation.61 | convolution fusion | flops 3222798336 | bytes 14155776 | tf_op jit(solution)/shard_map/dot_general | solution.py:53
  96.9 5.4 %convolution_convert_fusion = bf16[512,6144]{1,0:T(8,128)(2,1)} fusion(bf16[512,512]{1,0:T(8,128)(2,1)S(1)} %fusion.49, bf16[1,512,6144]{2,1,0:T(8,128)(2,1)S(1)} %bitcast.124), kind=kOutput, calls=%fused_computation.8 | convolution fusion | flops 3224371200 | bytes 13107200 | tf_op jit(solution)/shard_map/dot_general | solution.py:55
  102.6 2.7 fusion.28
  107.6 38.4 %all-gather.8.cloned.1.call-done = bf16[512,6144]{1,0:T(8,128)(2,1)} async-done(((bf16[32,6144]{1,0:T(8,128)(2,1)}), bf16[512,6144]{1,0:T(8,128)(2,1)}) %all-gather.8.cloned.1.call-update) | async-done | bytes 6291472 | tf_op jit(solution)/shard_map/all_gather | solution.py:122
  146.0 9.1 %fusion.5 = f32[512,512]{1,0:T(8,128)} fusion(bf16[512,6144]{1,0:T(8,128)(2,1)} %all-gather.8.cloned.1.call-done, bf16[1,6144,512]{2,1,0:T(8,128)(2,1)} %param.20), kind=kOutput, calls=%fused_computation.15 | convolution fusion | flops 3221225472 | bytes 13631488 | tf_op jit(solution)/shard_map/dot_general | solution.py:61
  155.1 5.6 %fusion.11 = f32[512,512]{1,0:T(8,128)S(1)} fusion(bf16[512,6144]{1,0:T(8,128)(2,1)S(1)} %copy-done.10, bf16[1,6144,512]{2,1,0:T(8,128)(2,1)} %param.19), kind=kOutput, calls=%fused_computation.21 | convolution fusion | flops 3221225472 | bytes 13631488 | tf_op jit(solution)/shard_map/dot_general | solution.py:60
  160.7 48.5 %all-gather.6.cloned.1.call-done = bf16[512,6144]{1,0:T(8,128)(2,1)} async-done(((bf16[32,6144]{1,0:T(8,128)(2,1)}), bf16[512,6144]{1,0:T(8,128)(2,1)}) %all-gather.6.cloned.1.call-update) | async-done | bytes 6291472 | tf_op jit(solution)/shard_map/all_gather | solution.py:123
  209.2 9.4 %multiply_reduce_fusion = (bf16[512]{0:T(512)(128)(2,1)S(1)}, f32[512,512]{1,0:T(8,128)}) fusion(f32[512,512]{1,0:T(8,128)} %fusion.5, f32[512,512]{1,0:T(8,128)S(1)} %fusion.11, bf16[512,6144]{1,0:T(8,128)(2,1)} %all-gather.6.cloned.1.call-done, bf16[1,512,6144]{2,1,0:T(8,128)(2,1)} %param.21), kind=kOutput, calls=%fused_computation.62 | convolution fusion | flops 3223584256 | bytes 15729664 | tf_op jit(solution)/shard_map/dot_general | solution.py:65
  218.7 32.1 %all-reduce.6 = (bf16[512]{0:T(512)(128)(2,1)S(1)}, bf16[512]{0:T(512)(128)(2,1)S(1)}) all-reduce(bf16[512]{0:T(512)(128)(2,1)S(1)} %get-tuple-element.32, bf16[512]{0:T(512)(128)(2,1)S(1)} %dynamic-update-slice), channel_id=4, replica_groups=mesh['section'=8,'expert'=16] {'expert'}, use_global_device_ids=true, to_apply=%region_15.18.clone | all-reduce | flops 1024 | bytes 4096
  250.8 11.9 %fusion.9 = f32[512,6144]{1,0:T(8,128)} fusion(bf16[1,6144,512]{2,1,0:T(8,128)(2,1)} %param.19, f32[512,512]{1,0:T(8,128)S(1)} %fusion.11, f32[512,512]{1,0:T(8,128)} %fusion.5, f32[512,512]{1,0:T(8,128)} %get-tuple-element.33, f32[512]{0:T(512)S(1)} %convert_element_type.98), kind=kOutput, calls=%fused_computation.19 | convolution fusion | flops 3224109056 | bytes 22022144 | tf_op jit(solution)/shard_map/dot_general | solution.py:75
  262.7 13.0 %add_convert_fusion = bf16[512,6144]{1,0:T(8,128)(2,1)} fusion(f32[512,6144]{1,0:T(8,128)} %fusion.9, bf16[1,6144,512]{2,1,0:T(8,128)(2,1)} %param.20, f32[512,512]{1,0:T(8,128)} %get-tuple-element.33, f32[512]{0:T(512)S(1)} %convert_element_type.98, f32[512,512]{1,0:T(8,128)S(1)} %fusion.11), kind=kOutput, calls=%fused_computation.7 | convolution fusion | flops 3229351936 | bytes 27265024 | tf_op jit(solution)/shard_map/dot_general | solution.py:76
  277.1 2.7 fusion.36
  280.1 1.5 gather_fusion.1
  281.6 10.9 %reduce-scatter.3.cloned.1.call-done = bf16[32,6144]{1,0:T(8,128)(2,1)} async-done(((bf16[512,6144]{1,0:T(8,128)(2,1)}), bf16[32,6144]{1,0:T(8,128)(2,1)}) %reduce-scatter.3.cloned.1.call-update) | async-done | bytes 393232 | tf_op jit(solution)/shard_map/reduce_scatter | solution.py:118
  293.6 3.2 gather_fusion.3
  296.8 4.1 fusion.41
  300.9 3.5 collective-permute-start
  304.3 72.8 %reduce-scatter.5.cloned.1.call-done = bf16[32,6144]{1,0:T(8,128)(2,1)} async-done(((bf16[512,6144]{1,0:T(8,128)(2,1)}), bf16[32,6144]{1,0:T(8,128)(2,1)}) %reduce-scatter.5.cloned.1.call-update) | async-done | bytes 393232 | tf_op jit(solution)/shard_map/reduce_scatter | solution.py:130
  378.2 3.2 gather_fusion.6
  381.3 5.2 %fusion.25 = (f32[128]{0:T(128)S(1)}, f32[128,6144]{1,0:T(8,128)S(1)}) fusion(bf16[1,128,6144]{2,1,0:T(8,128)(2,1)S(1)} %copy-done.1, f32[6144]{0:T(1024)S(1)} %bitcast.117, f32[128,8]{0,1:T(8,128)S(1)} %select_reduce_fusion.2, f32[1,6144,8]{1,2,0:T(8,128)S(1)} %copy-done, f32[128,6144]{1,0:T(8,128)} %gather_fusion.6, pred[128]{0:T(512)(128)(4,1)S(1)} %get-tuple-element.15), kind=kOutput, calls=%fused_computation.40 | convolution fusion | flops 80215936 | bytes 8090240 | tf_op jit(solution)/shard_map/transpose(jvp())/dot_general | solution.py:19
  387.5 2.4 collective-permute-start.1
  389.9 19.2 %collective-permute-done.1 = bf16[1,128,6144]{2,1,0:T(8,128)(2,1)S(1)} collective-permute-done((bf16[1,128,6144]{2,1,0:T(8,128)(2,1)S(1)}, bf16[1,128,6144]{2,1,0:T(8,128)(2,1)S(1)}, u32[]{:S(2)}, u32[]{:S(2)}) %collective-permute-start.1) | collective-permute-done | bytes 1572896 | tf_op jit(solution)/shard_map/ppermute | solution.py:13
  409.1 2.7 copy.77
  (87 shorter events, 10.8 us)
Async XLA Ops:
  7.2 95.4 %copy-start = (f32[1,6144,8]{1,2,0:T(8,128)S(1)}, f32[1,6144,8]{1,2,0:T(8,128)}, u32[]{:S(2)}) copy-start(f32[1,6144,8]{1,2,0:T(8,128)} %param.22) | copy-start | bytes 589828
  7.2 4.4 %copy-start.1 = (bf16[1,128,6144]{2,1,0:T(8,128)(2,1)S(1)}, bf16[1,128,6144]{2,1,0:T(8,128)(2,1)}, u32[]{:S(2)}) copy-start(bf16[1,128,6144]{2,1,0:T(8,128)(2,1)} %param.15) | copy-start | bytes 4718596
  7.2 4.9 %copy-start.6 = (f32[1,6144]{1,0:T(1,128)S(1)}, f32[1,6144]{1,0:T(1,128)}, u32[]{:S(2)}) copy-start(f32[1,6144]{1,0:T(1,128)} %param.23) | copy-start | bytes 73732
  7.2 75.0 %all-gather.4.cloned.1.call-start = ((), (), s32[]{:S(2)}) async-start(), calls=%async_computation.2 | async-start | bytes 6684672 | tf_op jit(solution)/shard_map/all_gather | solution.py:116
  9.6 2.5 copy-start.4
  15.7 5.6 %copy-start.2 = (bf16[1,128,6144]{2,1,0:T(8,128)(2,1)S(1)}, bf16[1,128,6144]{2,1,0:T(8,128)(2,1)}, u32[]{:S(2)}) copy-start(bf16[1,128,6144]{2,1,0:T(8,128)(2,1)} %param.16) | copy-start | bytes 4718596
  17.7 128.4 %all-gather.8.cloned.1.call-start = ((), (), s32[]{:S(2)}) async-start(), calls=%async_computation.5 | async-start | bytes 6684672 | tf_op jit(solution)/shard_map/all_gather | solution.py:122
  25.0 184.2 %all-gather.6.cloned.1.call-start = ((), (), s32[]{:S(2)}) async-start(), calls=%async_computation.4 | async-start | bytes 6684672 | tf_op jit(solution)/shard_map/all_gather | solution.py:123
  25.8 266.8 %reduce-scatter.3.cloned.1.call-start = ((), (), s32[]{:S(2)}) async-start(), calls=%async_computation.3 | async-start | bytes 6684672 | tf_op jit(solution)/shard_map/reduce_scatter | solution.py:118
  82.2 8.2 %copy-start.11 = (bf16[512,6144]{1,0:T(8,128)(2,1)S(1)}, bf16[512,6144]{1,0:T(8,128)(2,1)}, u32[]{:S(2)}) copy-start(bf16[512,6144]{1,0:T(8,128)(2,1)} %all-gather.4.cloned.1.call-done) | copy-start | bytes 18874372
  82.2 14.6 %slice-start = ((s8[6291456]{0:T(1024)(128)(4,1)}), s8[4194304]{0:T(1024)(128)(4,1)S(1)}, s32[]{:S(2)}) async-start(s8[6291456]{0:T(1024)(128)(4,1)} %bitcast.123), calls=%async_computation.7 | async-start | bytes 8388608
  90.4 6.4 %slice-start.1 = ((s8[6291456]{0:T(1024)(128)(4,1)}), s8[2097152]{0:T(1024)(128)(4,1)S(1)}, s32[]{:S(2)}) async-start(s8[6291456]{0:T(1024)(128)(4,1)} %bitcast.123), calls=%async_computation.8 | async-start | bytes 4194304
  102.3 3.0 copy-start.7
  102.3 3.8 copy-start.9
  102.3 274.8 %reduce-scatter.5.cloned.1.call-start = ((), (), s32[]{:S(2)}) async-start(), calls=%async_computation.6 | async-start | bytes 6684672 | tf_op jit(solution)/shard_map/reduce_scatter | solution.py:130
  146.0 9.1 %copy-start.10 = (bf16[512,6144]{1,0:T(8,128)(2,1)S(1)}, bf16[512,6144]{1,0:T(8,128)(2,1)}, u32[]{:S(2)}) copy-start(bf16[512,6144]{1,0:T(8,128)(2,1)} %all-gather.8.cloned.1.call-done) | copy-start | bytes 18874372
  275.7 1.4 copy-start.5
  275.7 4.1 copy-start.8
  300.9 89.0 %collective-permute-start = (bf16[1,128,6144]{2,1,0:T(8,128)(2,1)}, bf16[1,128,6144]{2,1,0:T(8,128)(2,1)}, u32[]{:S(2)}, u32[]{:S(2)}) collective-permute-start(bf16[1,128,6144]{2,1,0:T(8,128)(2,1)} %fusion.41), channel_id=1, source_target_pairs={{0,16},{16,32},{32,48},{48,64},{64,80},{80,96},{96,112},{112,0},{1... | collective-permute-start | bytes 4718600 | tf_op jit(solution)/shard_map/ppermute | solution.py:13
  381.3 5.2 %copy-start.3 = (bf16[1,128,6144]{2,1,0:T(8,128)(2,1)S(1)}, bf16[1,128,6144]{2,1,0:T(8,128)(2,1)}, u32[]{:S(2)}) copy-start(bf16[1,128,6144]{2,1,0:T(8,128)(2,1)} %param.16) | copy-start | bytes 4718596
  387.5 21.6 %collective-permute-start.1 = (bf16[1,128,6144]{2,1,0:T(8,128)(2,1)S(1)}, bf16[1,128,6144]{2,1,0:T(8,128)(2,1)S(1)}, u32[]{:S(2)}, u32[]{:S(2)}) collective-permute-start(bf16[1,128,6144]{2,1,0:T(8,128)(2,1)S(1)} %fusion.40), channel_id=1, source_target_pairs={{0,112},{16,0},{32,16},{48,32},{64,48},{80,64},{96,80},{112,96},{1... | collective-permute-start | bytes 4718600 | tf_op jit(solution)/shard_map/ppermute | solution.py:13
Sparse Core Ops, SparseCore 0:
  17.8 64.4 all-gather.3
  85.0 60.9 all-gather.7
  148.2 60.9 all-gather.5
  212.5 80.0 reduce-scatter.2
  295.8 81.2 reduce-scatter.4
where the time goes:
time: 420 us; the launch traced here: 419 us
  waiting for transfers between devices  247 us (59%)
  matrix products  79.7 us (19%)
  blocking collectives  32.1 us (8%)
  local copies, waits for them, and re-layouts  20.8 us (5%)
  other arithmetic  18.1 us (4%)
  between operations  15.5 us (4%)
  starting transfers between devices  6.29 us (1%)
    reduce_scatter x1, waiting for transfers between devices, local(): lax.psum_scatter(row_part.astype(jnp.float32).astype(jnp.bfloat16), 'expe...  72.8 us
    all_gather x1, waiting for transfers between devices, local(): gathered_f = lax.all_gather(send_f, 'expert', axis=0, tiled=True)  56.4 us
    all_gather x1, waiting for transfers between devices, local(): lax.all_gather(send_u, 'expert', axis=0, tiled=True)  48.5 us
    all_gather x1, waiting for transfers between devices, local(): lax.all_gather(send_h, 'expert', axis=0, tiled=True)  38.4 us
    unnamed x1, blocking collectives  32.1 us
    ppermute x2, waiting for transfers between devices, shifted(): return lax.ppermute(value, axis, pairs)  19.2 us
    dot_general x1, matrix products, backward_part(): lax.dot_general(up_cot, up_cols, last_dims, preferred_element_type=jnp.fl...  13 us
    dot_general x1, matrix products, backward_part(): lax.dot_general(gate_cot, gate_cols, last_dims, preferred_element_type=jn...  11.9 us
  transfers between devices with their start and end apart: 7, of which 6 were waited for; matrix products, arithmetic and copies ran while one was open for 25% of the time, Pallas kernels for 0%

commit v1 on v0

v1 whole, which is shorter than its diff:
```python
import functools

import jax
import jax.numpy as jnp
from jax import lax
from jax.experimental import pallas as pl
from jax.experimental.pallas import tpu as pltpu
from jax.sharding import PartitionSpec as P

EPS = 1e-05
NC = 6
CAP = 32
NS = 4
LEAD = 3
F32 = jnp.float32
BF16 = jnp.bfloat16
MESH = pl.DeviceIdType.MESH
HI = lax.Precision.HIGHEST
LAST = (((1,), (1,)), ((), ()))


def chosen(routes_t):
    tok = routes_t.shape[1]
    named = jnp.max((routes_t == 0).astype(F32), axis=0, keepdims=True)
    before = lax.broadcasted_iota(jnp.int32, (tok, tok), 0) < lax.broadcasted_iota(jnp.int32, (tok, tok), 1)
    wide = jnp.broadcast_to(named, (8, tok)).astype(BF16)
    rank = jnp.dot(wide, before.astype(F32).astype(BF16), preferred_element_type=F32)[0:1]
    slot = lax.broadcasted_iota(jnp.int32, (CAP, tok), 0).astype(F32)
    return jnp.where((slot == rank) & (named > 0.5), 1.0, 0.0).astype(BF16)


def prologue_kernel(act, saved, grad, rt_f, rt_b, router_t, gain, send, xf, xb, stats):
    width = send.shape[-1]
    depth = act.shape[1]

    def pick(onehot, source, c):
        return jnp.dot(onehot, source[:, c * width:(c + 1) * width], preferred_element_type=F32)

    def halves(value):
        return value.reshape(2, 16, width)

    def experts(onehot, routes):
        wide = jnp.concatenate([routes[...].astype(F32), jnp.zeros((6, routes.shape[1]), F32)], axis=0)
        both = lax.dot_general(onehot, wide.astype(BF16), LAST, preferred_element_type=F32)
        return both[:, 0:1], both[:, 1:2]

    pick_f = chosen(rt_f[...])
    pick_b = chosen(rt_b[...])
    for c in range(NC):
        send[c] = halves(pick(pick_b, grad, c).astype(BF16))

    def route(onehot, source, rows, routes, base):
        total = jnp.zeros((CAP, 1), F32)
        for c in range(NC):
            x = pick(onehot, source, c)
            rows[c] = halves(x.astype(BF16))
            total = total + jnp.sum(x * x, axis=1, keepdims=True)
        inverse = lax.rsqrt(total / depth + EPS)
        logits = jnp.zeros((CAP, 8), F32)
        for c in range(NC):
            cols = slice(c * width, (c + 1) * width)
            normed = rows[c].reshape(CAP, width).astype(F32) * inverse * gain[:, cols]
            send[base + c] = halves(normed.astype(BF16))
            logits = logits + lax.dot_general(
                normed, router_t[:, cols], LAST, precision=HI, preferred_element_type=F32
            )
        first, second = experts(onehot, routes)
        ids = lax.broadcasted_iota(jnp.int32, (CAP, 8), 1).astype(F32)
        picked1 = jnp.sum(jnp.where(ids == first, logits, 0.0), axis=1, keepdims=True)
        picked2 = jnp.sum(jnp.where(ids == second, logits, 0.0), axis=1, keepdims=True)
        share = jax.nn.sigmoid(picked1 - picked2)
        on1 = jnp.where(first == 0.0, 1.0, 0.0)
        on2 = jnp.where(second == 0.0, 1.0, 0.0)
        weight = share * on1 + (1.0 - share) * on2
        slope_scale = (on1 - on2) * share * (1.0 - share)
        return weight, inverse, slope_scale, first, second

    weight_f = route(pick_f, act, xf, rt_f, NC)[0]
    weight_b, inv_b, scale_b, first_b, second_b = route(pick_b, saved, xb, rt_b, 2 * NC)
    lane = lax.broadcasted_iota(jnp.int32, (CAP, 128), 1)
    table = jnp.zeros((CAP, 128), F32)
    for k, col in enumerate(
        (weight_f, weight_b.astype(BF16).astype(F32), inv_b, scale_b, first_b, second_b)
    ):
        table = jnp.where(lane == k, col, table)
    stats[...] = table


def main_kernel(
    send, xf, xb, stats, router_t, gain, rt_f, rt_b, act, grad, w_gate, w_up, w_down,
    rows_f, rows_b, rt_f2, rt_b2, act2, grad2,
    gath, gw, uw, dw, gacc, uacc, bacc, activ, gcot, ucot,
    part, r1, r2, q, r3, r4, gd, newf, newb, dots, slope, slope_in,
    ag_s1, ag_r1, ag_s, ag_r, rs_s, rs_r, sl_s, sl_r, w_sem, pass_s, pass_r, row_s, row_r,
):
    width = send.shape[-1]
    half_w = width // 2
    hid = gacc.shape[1]
    rows = gacc.shape[0]
    depth = gain.shape[1]
    n_ag, n_rs = 3 * NC, 2 * NC
    t_rs = n_ag
    n_sec = lax.axis_size("section")

    sec = lax.axis_index("section")
    ex = lax.axis_index("expert")
    y, z = ex // 4, ex % 4

    def turn(v, k):
        return (v + k + 4) % 4

    def dev_y(d):
        return (sec, turn(y, d) * 4 + z)

    def dev_z(d):
        return (sec, y * 4 + turn(z, d))

    sec_next = ((sec + 1) % n_sec, ex)
    sec_prev = ((sec + n_sec - 1) % n_sec, ex)
    DIRS = (1, -1)

    barrier = pltpu.get_barrier_semaphore()
    for dev in (dev_y(1), dev_y(-1), dev_z(1), dev_z(-1), sec_next, sec_prev):
        pl.semaphore_signal(barrier, inc=1, device_id=dev, device_id_type=MESH)

    def weight_copies(c):
        span = pl.ds(c * width, width)
        return (
            pltpu.make_async_copy(w_down.at[:, span], dw.at[c], w_sem.at[0, c]),
            pltpu.make_async_copy(w_gate.at[span, :], gw.at[c], w_sem.at[1, c]),
            pltpu.make_async_copy(w_up.at[span, :], uw.at[c], w_sem.at[2, c]),
        )

    own = pltpu.make_async_copy(send, gath.at[:, y, z], w_sem.at[3, 0])
    own.start()
    for c in range(NC):
        weight_copies(c)[0].start()
    for c in range(NC):
        weight_copies(c)[1].start()
        weight_copies(c)[2].start()

    def msg(src, dst, arrive, ssem, rsem, dev):
        def copy(target):
            return pltpu.make_async_remote_copy(
                src_ref=src, dst_ref=target, send_sem=ssem, recv_sem=rsem,
                device_id=dev, device_id_type=MESH,
            )

        def start():
            copy(dst).start()

        def finish():
            done = copy(arrive)
            done.wait_send()
            done.wait_recv()

        return start, finish

    def start_all(messages):
        for start, _ in messages:
            start()

    def finish_all(messages):
        for _, finish in messages:
            finish()

    COLS = (slice(0, half_w), slice(half_w, width))
    PAIR = (slice(0, 2), slice(2, 4))
    ALL = slice(0, 4)

    def ag_pos(h):
        return ((y, z, dev_y, dev_z), (z, y, dev_z, dev_y))[h]

    def g_at(n, fa, sa, h):
        return gath.at[n, fa, sa, h] if h == 0 else gath.at[n, sa, fa, h]

    def g_cols(n, fa, sa, h, cols):
        if h == 0:
            return gath.at[n, fa, sa, h, :, cols]
        return gath.at[n, sa, fa, h, :, cols]

    def ag1(n):
        out = []
        slot = n % 8
        for h in range(2):
            f, s, first, _ = ag_pos(h)
            for i, d in enumerate(DIRS):
                out.append(msg(send.at[n, h], g_at(n, f, s, h), g_at(n, turn(f, -d), s, h),
                               ag_s1.at[h, i, slot], ag_r1.at[h, i, slot], first(d)))
        return out

    def ag2(n):
        out = []
        slot = n % NS
        for h in range(2):
            f, s, first, _ = ag_pos(h)
            for i, d in enumerate(DIRS):
                src = g_cols(n, turn(f, -d), s, h, COLS[i])
                out.append(msg(src, src, g_cols(n, turn(f, 2), s, h, COLS[i]),
                               ag_s.at[0, h, i, slot], ag_r.at[0, h, i, slot], first(d)))
        return out

    def ag3(n):
        out = []
        slot = n % NS
        for h in range(2):
            f, s, _, second = ag_pos(h)
            for i, d in enumerate(DIRS):
                src = g_at(n, ALL, s, h)
                out.append(msg(src, src, g_at(n, ALL, turn(s, -d), h),
                               ag_s.at[1, h, i, slot], ag_r.at[1, h, i, slot], second(d)))
        return out

    def ag4(n):
        out = []
        slot = n % NS
        for h in range(2):
            f, s, _, second = ag_pos(h)
            for i, d in enumerate(DIRS):
                src = g_at(n, PAIR[i], turn(s, -d), h)
                out.append(msg(src, src, g_at(n, PAIR[i], turn(s, 2), h),
                               ag_s.at[2, h, i, slot], ag_r.at[2, h, i, slot], second(d)))
        return out

    def rs_pos(h):
        return ((z, y, dev_z, dev_y), (y, z, dev_y, dev_z))[h]

    def p_idx(slot, fa, sa, h):
        return (slot, sa, fa, h) if h == 0 else (slot, fa, sa, h)

    def rs1(m):
        out = []
        slot = m % NS
        for h in range(2):
            f, s, first, _ = rs_pos(h)
            for i, d in enumerate(DIRS):
                into = r1.at[h, i, slot]
                out.append(msg(part.at[p_idx(slot, turn(f, 2), PAIR[i], h)], into, into,
                               rs_s.at[0, h, i, slot], rs_r.at[0, h, i, slot], first(d)))
        return out

    def rs2(m):
        out = []
        slot = m % NS
        for h in range(2):
            f, s, first, _ = rs_pos(h)
            for i, d in enumerate(DIRS):
                into = r2.at[h, i, slot]
                out.append(msg(part.at[p_idx(slot, turn(f, d), ALL, h)], into, into,
                               rs_s.at[1, h, i, slot], rs_r.at[1, h, i, slot], first(d)))
        return out

    def rs3(m):
        out = []
        slot = m % NS
        for h in range(2):
            f, s, _, second = rs_pos(h)
            for i, d in enumerate(DIRS):
                into = r3.at[h, i, slot]
                out.append(msg(q.at[h, slot, turn(s, 2), :, COLS[i]], into, into,
                               rs_s.at[2, h, i, slot], rs_r.at[2, h, i, slot], second(d)))
        return out

    def rs4(m):
        out = []
        slot = m % NS
        for h in range(2):
            f, s, _, second = rs_pos(h)
            for i, d in enumerate(DIRS):
                into = r4.at[h, i, slot]
                out.append(msg(q.at[h, slot, turn(s, d)], into, into,
                               rs_s.at[3, h, i, slot], rs_r.at[3, h, i, slot], second(d)))
        return out

    def add1(m):
        slot = m % NS
        for h in range(2):
            f = rs_pos(h)[0]
            for i, d in enumerate(DIRS):
                at = p_idx(slot, turn(f, d), PAIR[i], h)
                part[at] = (part[at].astype(F32) + r1[h, i, slot].astype(F32)).astype(BF16)

    def add2(m):
        slot = m % NS
        for h in range(2):
            f = rs_pos(h)[0]
            mine = part[p_idx(slot, f, ALL, h)].astype(F32)
            q[h, slot] = (mine + r2[h, 0, slot].astype(F32) + r2[h, 1, slot].astype(F32)).astype(BF16)

    def add3(m):
        slot = m % NS
        for h in range(2):
            s = rs_pos(h)[1]
            for i, d in enumerate(DIRS):
                to = turn(s, d)
                q[h, slot, to, :, COLS[i]] = (
                    q[h, slot, to, :, COLS[i]].astype(F32) + r3[h, i, slot].astype(F32)
                ).astype(BF16)

    def summed(m, h):
        slot = m % NS
        s = rs_pos(h)[1]
        return (
            q[h, slot, s].astype(F32) + r4[h, 0, slot].astype(F32) + r4[h, 1, slot].astype(F32)
        )

    def sl_msgs(k, stage):
        axis_dev = (dev_z, dev_y)[k]
        if stage == 0:
            return [
                msg(slope.at[k], slope_in.at[k, i], slope_in.at[k, i],
                    sl_s.at[k, i], sl_r.at[k, i], axis_dev(d))
                for i, d in enumerate(DIRS)
            ]
        return [
            msg(slope_in.at[k, 0], slope_in.at[k, 2], slope_in.at[k, 2],
                sl_s.at[k, 2], sl_r.at[k, 2], axis_dev(1))
        ]

    def sl_sum(k):
        slope[k + 1] = slope[k] + slope_in[k, 0] + slope_in[k, 1] + slope_in[k, 2]

    def pass_msgs():
        out = []
        for i, (src, dst, dev) in enumerate(
            ((act, act2, sec_next), (grad, grad2, sec_prev), (rt_f, rt_f2, sec_next), (rt_b, rt_b2, sec_prev))
        ):
            out.append(msg(src, dst, dst, pass_s.at[i], pass_r.at[i], dev))
        return out

    row_f_msg = msg(newf, rows_f, rows_f, row_s.at[NC], row_r.at[NC], sec_next)

    def row_b_msg(c):
        return msg(newb.at[c], rows_b.at[c], rows_b.at[c], row_s.at[c], row_r.at[c], sec_prev)

    def lhs(n):
        return gath[n].reshape(rows, width)

    def fwd_rows(i, _):
        span = pl.ds(i * 64, 64)
        g = gacc[span, :]
        activ[span, :] = (g * jax.nn.sigmoid(g) * uacc[span, :]).astype(BF16)
        gacc[span, :] = jnp.zeros((64, hid), F32)
        uacc[span, :] = jnp.zeros((64, hid), F32)
        return 0

    def bwd_rows(i, _):
        span = pl.ds(i * 128, 128)
        g = gacc[span, :]
        u = uacc[span, :]
        back = bacc[span, :]
        sig = jax.nn.sigmoid(g)
        silu = g * sig
        prod = (silu * u).astype(BF16).astype(F32) * back
        high = prod.astype(BF16)
        low = (prod - high.astype(F32)).astype(BF16)
        ones = jnp.ones((8, hid), BF16)
        slope[0, :, span] = lax.dot_general(
            ones, high, LAST, preferred_element_type=F32
        ) + lax.dot_general(ones, low, LAST, preferred_element_type=F32)
        gcot[span, :] = (back * u * sig * (1.0 + g * (1.0 - sig))).astype(BF16)
        ucot[span, :] = (back * silu).astype(BF16)
        return 0

    def col(h, k):
        return stats[h * 16:(h + 1) * 16, k:k + 1]

    def finish_forward(m):
        for h in range(2):
            newf[m, h] = (xf[m, h].astype(F32) + col(h, 0) * summed(m, h)).astype(BF16)

    def finish_backward(m):
        c = m - NC
        span = pl.ds(pl.multiple_of(c * width, 128), width)
        router_c = router_t[:, span]
        gain_c = gain[:, span]
        ids = lax.broadcasted_iota(jnp.int32, (16, 8), 1).astype(F32)
        place = lax.broadcasted_iota(jnp.int32, (16, rows), 1)
        row = lax.broadcasted_iota(jnp.int32, (16, rows), 0)
        for h in range(2):
            mine = place == row + (ex * CAP + h * 16)
            cot = jnp.sum(jnp.where(mine, slope[2, 0:1, :], 0.0), axis=1, keepdims=True) * col(h, 3)
            both = jnp.where(ids == col(h, 4), 1.0, 0.0) - jnp.where(ids == col(h, 5), 1.0, 0.0)
            dlog = cot * both
            dn = col(h, 1) * summed(m, h)
            for e in range(8):
                dn = dn + dlog[:, e:e + 1] * router_c[e:e + 1, :]
            dn = dn * gain_c
            gd[c, h] = dn
            line = jnp.sum(dn * xb[c, h].astype(F32), axis=1, keepdims=True)
            at = slice(h * 16, (h + 1) * 16)
            dots[at, :] = dots[at, :] + jnp.broadcast_to(line, (16, 128))

    gacc[...] = jnp.zeros_like(gacc)
    uacc[...] = jnp.zeros_like(uacc)
    bacc[...] = jnp.zeros_like(bacc)
    dots[...] = jnp.zeros_like(dots)

    pl.semaphore_wait(barrier, 6)
    for n in range(LEAD):
        start_all(ag1(n))
    start_all(pass_msgs())
    own.wait()

    def when_in(value, low, high):
        return pl.when(jnp.logical_and(value >= low, value < high))

    def step(t, _):
        @when_in(t, 0, n_ag - LEAD)
        def _():
            start_all(ag1(t + LEAD))

        @when_in(t, 1, n_ag + 1)
        def _():
            finish_all(ag1(t - 1))
            start_all(ag2(t - 1))

        @when_in(t, 2, n_ag + 2)
        def _():
            finish_all(ag2(t - 2))
            start_all(ag3(t - 2))

        @when_in(t, 3, n_ag + 3)
        def _():
            finish_all(ag3(t - 3))
            start_all(ag4(t - 3))

        @when_in(t, 4, n_ag + 4)
        def _():
            finish_all(ag4(t - 4))

        r = t - t_rs

        @when_in(r, 0, n_rs)
        def _():
            start_all(rs1(r))

        @when_in(r, 1, n_rs + 1)
        def _():
            finish_all(rs1(r - 1))
            add1(r - 1)
            start_all(rs2(r - 1))

        @when_in(r, 2, n_rs + 2)
        def _():
            finish_all(rs2(r - 2))
            add2(r - 2)
            start_all(rs3(r - 2))

        @when_in(r, 3, n_rs + 3)
        def _():
            finish_all(rs3(r - 3))
            add3(r - 3)
            start_all(rs4(r - 3))

        @when_in(r, 4, n_rs + 4)
        def _():
            finish_all(rs4(r - 4))

        @when_in(r, 4, NC + 4)
        def _():
            finish_forward(r - 4)

        @pl.when(r == NC + 3)
        def _():
            row_f_msg[0]()

        @pl.when(t == n_ag + 4)
        def _():
            start_all(sl_msgs(0, 0))

        @pl.when(t == n_ag + 5)
        def _():
            finish_all(sl_msgs(0, 0))
            start_all(sl_msgs(0, 1))

        @pl.when(t == n_ag + 6)
        def _():
            finish_all(sl_msgs(0, 1))
            sl_sum(0)
            start_all(sl_msgs(1, 0))

        @pl.when(t == n_ag + 7)
        def _():
            finish_all(sl_msgs(1, 0))
            start_all(sl_msgs(1, 1))

        @pl.when(t == n_ag + 8)
        def _():
            finish_all(sl_msgs(1, 1))
            sl_sum(1)

        @when_in(r, NC + 4, n_rs + 4)
        def _():
            finish_backward(r - 4)

        n = t - 4

        @when_in(n, 0, NC)
        def _():
            weight_copies(n)[0].wait()
            bacc[...] += lax.dot_general(lhs(n), dw[n], LAST, preferred_element_type=F32)

        @when_in(n, NC, 2 * NC)
        def _():
            weight_copies(n - NC)[1].wait()
            weight_copies(n - NC)[2].wait()

        @when_in(n, NC, n_ag)
        def _():
            c = n % NC
            gacc[...] += jnp.dot(lhs(n), gw[c], preferred_element_type=F32)
            uacc[...] += jnp.dot(lhs(n), uw[c], preferred_element_type=F32)

        @pl.when(n == 2 * NC - 1)
        def _():
            lax.fori_loop(0, rows // 64, fwd_rows, 0)

        @pl.when(n == n_ag - 1)
        def _():
            lax.fori_loop(0, rows // 128, bwd_rows, 0)

        m = r + 1
        shape = part.shape[1:]

        @when_in(m, 0, NC)
        def _():
            part[m % NS] = jnp.dot(activ[...], dw[m], preferred_element_type=F32).astype(BF16).reshape(shape)

        @when_in(m, NC, n_rs)
        def _():
            c = m - NC
            value = lax.dot_general(gcot[...], gw[c], LAST, preferred_element_type=F32)
            value = value + lax.dot_general(ucot[...], uw[c], LAST, preferred_element_type=F32)
            part[m % NS] = value.astype(BF16).reshape(shape)

        return 0

    lax.fori_loop(0, t_rs + n_rs + 4, step, 0)

    def last(c, _):
        for h in range(2):
            inv = col(h, 2)
            coef = inv * inv * inv * dots[h * 16:(h + 1) * 16, 0:1] / depth
            change = inv * gd[c, h] - coef * xb[c, h].astype(F32)
            newb[c, h] = (send[c, h].astype(F32) + change).astype(BF16)
        row_b_msg(c)[0]()
        return 0

    lax.fori_loop(0, NC, last, 0)

    finish_all(pass_msgs())
    row_f_msg[1]()

    def drain(c, _):
        row_b_msg(c)[1]()
        return 0

    lax.fori_loop(0, NC, drain, 0)


def merge_kernel(rt_f, rt_b, act, grad, rows_f, rows_b, out_f, out_b):
    width = act.shape[-1]
    for routes, plain, rows, out in ((rt_f, act, rows_f, out_f), (rt_b, grad, rows_b, out_b)):
        onehot = chosen(routes[...])
        first = (((0,), (0,)), ((), ()))
        moved = lax.dot_general(onehot, rows[0].reshape(CAP, width), first, preferred_element_type=F32)
        held = lax.dot_general(onehot, jnp.ones((CAP, 128), BF16), first, preferred_element_type=F32)
        out[...] = jnp.where(held[:, 0:1] > 0.5, moved, plain[...].astype(F32)).astype(BF16)


def local(act_in, saved_in, grad_in, fwd_routes, bwd_routes, w_gate, w_up, w_down, router, norm_gain):
    act, saved, grad = act_in[0], saved_in[0], grad_in[0]
    rt_f, rt_b = fwd_routes[0].T, bwd_routes[0].T
    router_t = router[0].T
    tok, depth = act.shape
    width = depth // NC
    hid = w_gate.shape[2]
    rows = 16 * CAP
    sds = jax.ShapeDtypeStruct
    vmem = pl.BlockSpec(memory_space=pltpu.VMEM)
    anywhere = pl.BlockSpec(memory_space=pl.ANY)
    dma = pltpu.SemaphoreType.DMA
    row_shape = (NC, 2, 16, width)

    send, xf, xb, stats = pl.pallas_call(
        prologue_kernel,
        out_shape=(
            sds((3 * NC, 2, 16, width), BF16), sds(row_shape, BF16), sds(row_shape, BF16), sds((CAP, 128), F32),
        ),
        in_specs=[vmem] * 7,
        out_specs=(vmem,) * 4,
        compiler_params=pltpu.CompilerParams(vmem_limit_bytes=32 << 20),
    )(act, saved, grad, rt_f, rt_b, router_t, norm_gain)

    V = pltpu.VMEM
    rows_f, rows_b, rt_f2, rt_b2, act2, grad2 = pl.pallas_call(
        main_kernel,
        out_shape=(
            sds(row_shape, BF16), sds(row_shape, BF16),
            sds(rt_f.shape, jnp.int32), sds(rt_b.shape, jnp.int32),
            sds(act.shape, BF16), sds(grad.shape, BF16),
        ),
        in_specs=[vmem] * 8 + [anywhere] * 5,
        out_specs=(vmem,) * 4 + (anywhere,) * 2,
        scratch_shapes=[
            V((3 * NC, 4, 4, 2, 16, width), BF16),
            V((NC, width, hid), BF16), V((NC, width, hid), BF16), V((NC, hid, width), BF16),
            V((rows, hid), F32), V((rows, hid), F32), V((rows, hid), F32),
            V((rows, hid), BF16), V((rows, hid), BF16), V((rows, hid), BF16),
            V((NS, 4, 4, 2, 16, width), BF16),
            V((2, 2, NS, 2, 16, width), BF16), V((2, 2, NS, 4, 16, width), BF16),
            V((2, NS, 4, 16, width), BF16),
            V((2, 2, NS, 16, width // 2), BF16), V((2, 2, NS, 16, width), BF16),
            V(row_shape, F32), V(row_shape, BF16), V(row_shape, BF16), V((CAP, 128), F32),
            V((3, 8, rows), F32), V((2, 3, 8, rows), F32),
            dma((2, 2, 8)), dma((2, 2, 8)),
            dma((3, 2, 2, NS)), dma((3, 2, 2, NS)),
            dma((4, 2, 2, NS)), dma((4, 2, 2, NS)),
            dma((2, 3)), dma((2, 3)),
            dma((4, NC)), dma((4,)), dma((4,)), dma((NC + 1,)), dma((NC + 1,)),
        ],
        compiler_params=pltpu.CompilerParams(
            collective_id=0, has_side_effects=True, vmem_limit_bytes=67_000_000
        ),
    )(send, xf, xb, stats, router_t, norm_gain, rt_f, rt_b, act, grad, w_gate[0], w_up[0], w_down[0])

    whole = pl.BlockSpec(rt_f.shape, lambda c: (0, 0))
    columns = pl.BlockSpec((tok, width), lambda c: (0, c))
    slots = pl.BlockSpec((1, 2, 16, width), lambda c: (c, 0, 0, 0))
    out_f, out_b = pl.pallas_call(
        merge_kernel,
        grid=(NC,),
        out_shape=(sds(act.shape, BF16), sds(grad.shape, BF16)),
        in_specs=[whole, whole, columns, columns, slots, slots],
        out_specs=(columns, columns),
    )(rt_f2, rt_b2, act2, grad2, rows_f, rows_b)
    return (out_f[None], out_b[None])


def solution(mesh):
    in_specs = (
        P("section", "expert", None),
        P("section", "expert", None),
        P("section", "expert", None),
        P("section", "expert", None),
        P("section", "expert", None),
        P("section", None, "expert"),
        P("section", None, "expert"),
        P("section", "expert", None),
        P("section", None, None),
        P("section", None),
    )
    out_specs = (P("section", "expert", None), P("section", "expert", None))
    return jax.shard_map(local, mesh=mesh, in_specs=in_specs, out_specs=out_specs, check_vma=False)
```

time: 420 us -> 209 us (0.50)
  waiting for transfers between devices: 247 us -> 0 us
  Pallas kernels: 0 us -> 198 us
  matrix products: 79.7 us -> 0 us
  blocking collectives: 32.1 us -> 0 us
  other arithmetic: 18.1 us -> 0 us
  between operations: 15.5 us -> 0.67 us
  local copies, waits for them, and re-layouts: 20.8 us -> 10.3 us
  starting transfers between devices: 6.29 us -> 0 us
    pallas_call x0 -> x3, Pallas kernels: none -> 198 us  [the longest x1 188 us: local(): pl.pallas_call(main_kernel, out_shape=(sds(row_shape, BF16), sds(row_shap...]
    all_gather x3 -> x0, waiting for transfers between devices: 143 us -> none  [the longest x1 56.4 us: local(): gathered_f = lax.all_gather(send_f, 'expert', axis=0, tiled=True)]
    reduce_scatter x2 -> x0, waiting for transfers between devices: 83.7 us -> none  [the longest x1 72.8 us: local(): lax.psum_scatter(row_part.astype(jnp.float32).astype(jnp.bfloat16), 'expe...]
    dot_general x11 -> x0, matrix products: 79.7 us -> none  [the longest x1 13 us: backward_part(): lax.dot_general(up_cot, up_cols, last_dims, preferred_element_type=jnp.fl...]
    unnamed x1 -> x0, blocking collectives: 32.1 us -> none
    ppermute x2 -> x0, waiting for transfers between devices: 19.2 us -> none  [shifted(): return lax.ppermute(value, axis, pairs)]
    gather x7 -> x0, local copies, waits for them, and re-layouts: 15.2 us -> none  [the longest x3 7.84 us: unfill(): return jnp.take(padded, slot_of, axis=0)]
    ppermute x2 -> x0, starting transfers between devices: 5.91 us -> none  [shifted(): return lax.ppermute(value, axis, pairs)]
  transfers between devices with their start and end apart: 7 -> 0, of which waited for: 6 -> 0; matrix products, arithmetic and copies ran while one was open for 25% -> 0% of each run, Pallas kernels for 0% -> 0%
where the time goes in v1:
time: 209 us
  Pallas kernels  198 us (95%)
  local copies, waits for them, and re-layouts  10.3 us (5%)
    pallas_call x1, Pallas kernels, local(): pl.pallas_call(main_kernel, out_shape=(sds(row_shape, BF16), sds(row_shap...  188 us
    unnamed x22, local copies, waits for them, and re-layouts  10.3 us
    pallas_call x1, Pallas kernels, local(): pl.pallas_call(merge_kernel, grid=(NC,), out_shape=(sds(act.shape, BF16),...  7.25 us

profile of v1, /device:TPU:1, one launch (start us, length us, event | category | flops | bytes accessed | tf_op | source)
XLA Modules:
  0.0 208.6 jit_solution(8791050601460163870)
XLA Ops:
  0.6 0.0 copy-start
  0.6 1.4 copy-done
  2.0 0.0 copy-start.1
  2.0 1.4 copy-done.1
  3.4 0.0 copy-start.2
  3.5 1.4 copy-done.2
  4.9 0.0 copy-start.4
  4.9 0.9 copy-done.4
  5.8 0.0 copy-start.7
  5.8 0.7 copy-done.7
  6.5 0.0 copy-start.9
  6.5 0.7 copy-done.9
  7.2 0.0 copy-start.10
  7.2 0.7 copy-done.10
  7.9 2.6 %shard_map.113 = (bf16[18,2,16,1024]{3,2,1,0:T(8,128)(2,1)S(1)}, bf16[6,2,16,1024]{3,2,1,0:T(8,128)(2,1)S(1)}, bf16[6,2,16,1024]{3,2,1,0:T(8,128)(2,1)S(1)}, f32[32,128]{1,0:T(8,128)S(1)}) custom-call(bf16[128,6144]{1,0:T(8,128)(2,1)S(1)} %bitcast.18, bf16[128,6144]{1,0:T(8,128)(2,1)S(1)} %bitcast.21, bf16[128,6144]{1,0:T(8,128)(2,1)S(1)} %bitcast.20, ...), custom_call_target="tpu_custom_call" | custom-call | tf_op jit(solution)/shard_map/pallas_call | solution.py:586
  10.5 0.0 copy-start.3
  10.5 1.0 copy-done.3
  11.5 0.0 copy-start.5
  11.5 0.7 copy-done.5
  12.3 0.0 copy-start.6
  12.3 0.8 copy-done.6
  13.0 0.0 copy-start.8
  13.0 0.6 copy-done.8
  13.6 187.8 %shard_map.114 = (bf16[6,2,16,1024]{3,2,1,0:T(8,128)(2,1)}, bf16[6,2,16,1024]{3,2,1,0:T(8,128)(2,1)}, s32[2,128]{1,0:T(2,128)}, s32[2,128]{1,0:T(2,128)}, bf16[1...) custom-call(bf16[18,2,16,1024]{3,2,1,0:T(8,128)(2,1)} %copy-done.3, bf16[6,2,16,1024]{3,2,1,0:T(8,128)(2,1)} %copy-done.5, ...), custom_call_target="tpu_custom_call" | custom-call | tf_op jit(solution)/shard_map/pallas_call | solution.py:597
  201.4 7.3 %shard_map.115 = (bf16[128,6144]{1,0:T(8,128)(2,1)}, bf16[128,6144]{1,0:T(8,128)(2,1)}) custom-call(s32[2,128]{1,0:T(2,128)} %get-tuple-element.18.rt_f, s32[2,128]{1,0:T(2,128)} %get-tuple-element.19.rt_b, bf16[128,6144]{1,0:T(8,128)(2,1)} %get-tuple-element.20.act, bf16[128,6144]{1,0:T(8,128)(2,1)} %get-tuple-element.21.grad, ...), custom_call_target="tpu_custom_call" | custom-call | tf_op jit(solution)/shard_map/pallas_call | solution.py:631
Async XLA Ops:
  0.6 1.4 copy-start
  2.0 1.4 copy-start.1
  3.4 1.4 copy-start.2
  4.9 0.9 copy-start.4
  5.8 0.7 copy-start.7
  6.5 0.7 copy-start.9
  7.2 0.7 copy-start.10
  10.5 1.0 copy-start.3
  11.5 0.7 copy-start.5
  12.3 0.8 copy-start.6
  13.0 0.6 copy-start.8

commit v2 on v1

v2 whole, which is shorter than its diff:
```python
import functools

import jax
import jax.numpy as jnp
from jax import lax
from jax.experimental import pallas as pl
from jax.experimental.pallas import tpu as pltpu
from jax.sharding import PartitionSpec as P

EPS = 1e-05
NC = 4
MERGE = 2
CAP = 32
LAG = 2
NS = 2 * LAG + 1
NG = 8
F32 = jnp.float32
BF16 = jnp.bfloat16
MESH = pl.DeviceIdType.MESH
HI = lax.Precision.HIGHEST
LAST = (((1,), (1,)), ((), ()))


def chosen(routes_t):
    tok = routes_t.shape[1]
    named = jnp.max((routes_t == 0).astype(F32), axis=0, keepdims=True)
    before = lax.broadcasted_iota(jnp.int32, (tok, tok), 0) < lax.broadcasted_iota(jnp.int32, (tok, tok), 1)
    wide = jnp.broadcast_to(named, (8, tok)).astype(BF16)
    rank = jnp.dot(wide, before.astype(F32).astype(BF16), preferred_element_type=F32)[0:1]
    slot = lax.broadcasted_iota(jnp.int32, (CAP, tok), 0).astype(F32)
    onehot = jnp.where((slot == rank) & (named > 0.5), 1.0, 0.0).astype(BF16)
    return onehot, named


def main_kernel(
    act, saved, grad, rt_f, rt_b, router, norm_gain, w_gate, w_up, w_down,
    rows_f, rows_b, sel_f, sel_b, act2, grad2,
    source, routes, router_t, gain, xf, xb, stats, sel,
    gath, gw, uw, dw, gacc, uacc, bacc, activ, gcot, ucot,
    part, r1, r2, q, r3, r4, slope, slope_in,
    one_s, one_r, grp_s, grp_r, ag_s, ag_r, rs_s, rs_r, sl_s, sl_r,
    in_sem, small_sem, pass_s, pass_r, row_s, row_r,
):
    width = gath.shape[-1]
    half_w = width // 2
    hid = gacc.shape[1]
    rows = gacc.shape[0]
    depth = gain.shape[1]
    n_ag, n_rs = 3 * NC, 2 * NC
    t_rs = n_ag + 1
    n_sec = lax.axis_size("section")

    sec = lax.axis_index("section")
    ex = lax.axis_index("expert")
    y, z = ex // 4, ex % 4

    def turn(v, k):
        return (v + k + 4) % 4

    def dev_y(d):
        return (sec, turn(y, d) * 4 + z)

    def dev_z(d):
        return (sec, y * 4 + turn(z, d))

    sec_next = ((sec + 1) % n_sec, ex)
    sec_prev = ((sec + n_sec - 1) % n_sec, ex)
    DIRS = (1, -1)

    barrier = pltpu.get_barrier_semaphore()
    for dev in (dev_y(1), dev_y(-1), dev_z(1), dev_z(-1), sec_next, sec_prev):
        pl.semaphore_signal(barrier, inc=1, device_id=dev, device_id_type=MESH)

    def span(c):
        return pl.ds(c * width, width)

    def weight_copies(c):
        return (
            pltpu.make_async_copy(w_down.at[:, span(c)], dw.at[c], in_sem.at[0, c]),
            pltpu.make_async_copy(w_gate.at[span(c), :], gw.at[c], in_sem.at[1, c]),
            pltpu.make_async_copy(w_up.at[span(c), :], uw.at[c], in_sem.at[2, c]),
        )

    arrays = (grad, act, saved)

    def source_copy(k, c):
        return pltpu.make_async_copy(
            arrays[k].at[:, span(c)], source.at[:, span(c)], in_sem.at[3 + k, c]
        )

    small = [
        pltpu.make_async_copy(a, b, small_sem.at[i])
        for i, (a, b) in enumerate(
            ((rt_b, routes.at[1]), (rt_f, routes.at[0]), (norm_gain, gain), (router, router_t))
        )
    ]
    small[0].start()
    for c in range(NC):
        source_copy(0, c).start()
    for k in (1, 2, 3):
        small[k].start()

    def msg(src, dst, arrive, ssem, rsem, dev):
        def copy(target):
            return pltpu.make_async_remote_copy(
                src_ref=src, dst_ref=target, send_sem=ssem, recv_sem=rsem,
                device_id=dev, device_id_type=MESH,
            )

        def start():
            copy(dst).start()

        def finish():
            done = copy(arrive)
            done.wait_send()
            done.wait_recv()

        return start, finish

    def start_all(messages):
        for start, _ in messages:
            start()

    def finish_all(messages):
        for _, finish in messages:
            finish()

    COLS = (slice(0, half_w), slice(half_w, width))
    PAIR = (slice(0, 2), slice(2, 4))
    ALL = slice(0, 4)

    def ag_pos(h):
        return ((y, z, dev_y, dev_z), (z, y, dev_z, dev_y))[h]

    def g_at(n, fa, sa, h):
        return gath.at[n, fa, sa, h] if h == 0 else gath.at[n, sa, fa, h]

    def g_cols(n, fa, sa, h, cols):
        if h == 0:
            return gath.at[n, fa, sa, h, :, cols]
        return gath.at[n, sa, fa, h, :, cols]

    def one(stage, n):
        out = []
        for h in range(2):
            f, s, first, _ = ag_pos(h)
            for i, d in enumerate(DIRS):
                sems = (one_s.at[stage, h, i, n], one_r.at[stage, h, i, n], first(d))
                if stage == 0:
                    src = g_at(n, f, s, h)
                    out.append(msg(src, src, g_at(n, turn(f, -d), s, h), *sems))
                else:
                    src = g_cols(n, turn(f, -d), s, h, COLS[i])
                    out.append(msg(src, src, g_cols(n, turn(f, 2), s, h, COLS[i]), *sems))
        return out

    def group(stage, k):
        out = []
        lo, mid, hi = k * NC, k * NC + NC // 2, (k + 1) * NC
        for h in range(2):
            f, s, first, _ = ag_pos(h)
            for i, d in enumerate(DIRS):
                sems = (grp_s.at[k - 1, stage, h, i], grp_r.at[k - 1, stage, h, i], first(d))
                if stage == 0:
                    part_of = slice(lo, hi)
                    src = g_at(part_of, f, s, h)
                    out.append(msg(src, src, g_at(part_of, turn(f, -d), s, h), *sems))
                else:
                    part_of = (slice(lo, mid), slice(mid, hi))[i]
                    src = g_at(part_of, turn(f, -d), s, h)
                    out.append(msg(src, src, g_at(part_of, turn(f, 2), s, h), *sems))
        return out

    def ag3(n):
        out = []
        slot = n % NG
        for h in range(2):
            f, s, _, second = ag_pos(h)
            for i, d in enumerate(DIRS):
                src = g_at(n, ALL, s, h)
                out.append(msg(src, src, g_at(n, ALL, turn(s, -d), h),
                               ag_s.at[0, h, i, slot], ag_r.at[0, h, i, slot], second(d)))
        return out

    def ag4(n):
        out = []
        slot = n % NG
        for h in range(2):
            f, s, _, second = ag_pos(h)
            for i, d in enumerate(DIRS):
                src = g_at(n, PAIR[i], turn(s, -d), h)
                out.append(msg(src, src, g_at(n, PAIR[i], turn(s, 2), h),
                               ag_s.at[1, h, i, slot], ag_r.at[1, h, i, slot], second(d)))
        return out

    def rs_pos(h):
        return ((z, y, dev_z, dev_y), (y, z, dev_y, dev_z))[h]

    def p_idx(slot, fa, sa, h):
        return (slot, sa, fa, h) if h == 0 else (slot, fa, sa, h)

    def rs1(m):
        out = []
        slot = m % NS
        for h in range(2):
            f, s, first, _ = rs_pos(h)
            for i, d in enumerate(DIRS):
                into = r1.at[h, i, slot]
                out.append(msg(part.at[p_idx(slot, turn(f, 2), PAIR[i], h)], into, into,
                               rs_s.at[0, h, i, slot], rs_r.at[0, h, i, slot], first(d)))
        return out

    def rs2(m):
        out = []
        slot = m % NS
        for h in range(2):
            f, s, first, _ = rs_pos(h)
            for i, d in enumerate(DIRS):
                into = r2.at[h, i, slot]
                out.append(msg(part.at[p_idx(slot, turn(f, d), ALL, h)], into, into,
                               rs_s.at[1, h, i, slot], rs_r.at[1, h, i, slot], first(d)))
        return out

    def rs3(m):
        out = []
        slot = m % NS
        for h in range(2):
            f, s, _, second = rs_pos(h)
            for i, d in enumerate(DIRS):
                into = r3.at[h, i, slot]
                out.append(msg(q.at[h, slot, turn(s, 2), :, COLS[i]], into, into,
                               rs_s.at[2, h, i, slot], rs_r.at[2, h, i, slot], second(d)))
        return out

    def rs4(m):
        out = []
        slot = m % NS
        for h in range(2):
            f, s, _, second = rs_pos(h)
            for i, d in enumerate(DIRS):
                into = r4.at[h, i, slot]
                out.append(msg(q.at[h, slot, turn(s, d)], into, into,
                               rs_s.at[3, h, i, slot], rs_r.at[3, h, i, slot], second(d)))
        return out

    def add1(m):
        slot = m % NS
        for h in range(2):
            f = rs_pos(h)[0]
            for i, d in enumerate(DIRS):
                at = p_idx(slot, turn(f, d), PAIR[i], h)
                part[at] = (part[at].astype(F32) + r1[h, i, slot].astype(F32)).astype(BF16)

    def add2(m):
        slot = m % NS
        for h in range(2):
            f = rs_pos(h)[0]
            mine = part[p_idx(slot, f, ALL, h)].astype(F32)
            q[h, slot] = (mine + r2[h, 0, slot].astype(F32) + r2[h, 1, slot].astype(F32)).astype(BF16)

    def add3(m):
        slot = m % NS
        for h in range(2):
            s = rs_pos(h)[1]
            for i, d in enumerate(DIRS):
                to = turn(s, d)
                q[h, slot, to, :, COLS[i]] = (
                    q[h, slot, to, :, COLS[i]].astype(F32) + r3[h, i, slot].astype(F32)
                ).astype(BF16)

    def summed(m, h):
        slot = m % NS
        s = rs_pos(h)[1]
        return (
            q[h, slot, s].astype(F32) + r4[h, 0, slot].astype(F32) + r4[h, 1, slot].astype(F32)
        )

    def sl_msgs(k, stage):
        axis_dev = (dev_z, dev_y)[k]
        if stage == 0:
            return [
                msg(slope.at[k], slope_in.at[k, i], slope_in.at[k, i],
                    sl_s.at[k, i], sl_r.at[k, i], axis_dev(d))
                for i, d in enumerate(DIRS)
            ]
        return [
            msg(slope_in.at[k, 0], slope_in.at[k, 2], slope_in.at[k, 2],
                sl_s.at[k, 2], sl_r.at[k, 2], axis_dev(1))
        ]

    def sl_sum(k):
        slope[k + 1] = slope[k] + slope_in[k, 0] + slope_in[k, 1] + slope_in[k, 2]

    def pass_msgs(which):
        out = []
        for i, (src, dst, dev) in enumerate(
            ((act, act2, sec_next), (grad, grad2, sec_prev), (sel.at[0], sel_f, sec_next), (sel.at[1], sel_b, sec_prev))
        ):
            if i in which:
                out.append(msg(src, dst, dst, pass_s.at[i], pass_r.at[i], dev))
        return out

    row_f_msg = msg(xf, rows_f, rows_f, row_s.at[NC], row_r.at[NC], sec_next)

    def row_b_msg(c):
        return msg(xb.at[c], rows_b.at[c], rows_b.at[c], row_s.at[c], row_r.at[c], sec_prev)

    def lhs(n):
        return gath[n].reshape(rows, width)

    def fwd_rows(i, _):
        at = pl.ds(i * 64, 64)
        g = gacc[at, :]
        activ[at, :] = (g * jax.nn.sigmoid(g) * uacc[at, :]).astype(BF16)
        gacc[at, :] = jnp.zeros((64, hid), F32)
        uacc[at, :] = jnp.zeros((64, hid), F32)
        return 0

    def row_sums(value):
        high = value.astype(BF16)
        low = (value - high.astype(F32)).astype(BF16)
        ones = jnp.ones((8, hid), BF16)
        return lax.dot_general(ones, high, LAST, preferred_element_type=F32) + lax.dot_general(
            ones, low, LAST, preferred_element_type=F32
        )

    def bwd_rows(i, _):
        at = pl.ds(i * 128, 128)
        g = gacc[at, :]
        u = uacc[at, :]
        back = bacc[at, :]
        sig = jax.nn.sigmoid(g)
        silu = g * sig
        prod = (silu * u).astype(BF16).astype(F32) * back
        dgate = (back * u * sig * (1.0 + g * (1.0 - sig))).astype(BF16)
        dup = (back * silu).astype(BF16)
        gcot[at, :] = dgate
        ucot[at, :] = dup
        inner = dgate.astype(F32) * g + dup.astype(F32) * u
        upper = lax.broadcasted_iota(jnp.int32, (8, 128), 0) < 4
        slope[0, :, at] = jnp.where(upper, row_sums(prod), row_sums(inner))
        return 0

    def col(k, h, j):
        return stats[k, h * 16:(h + 1) * 16, j:j + 1]

    def finish_forward(m):
        for h in range(2):
            xf[m, h] = (xf[m, h].astype(F32) + col(0, h, 0) * summed(m, h)).astype(BF16)

    def finish_backward(m):
        c = m - NC
        at = pl.ds(pl.multiple_of(c * width, 128), width)
        router_c = router_t[:, at]
        gain_c = gain[:, at]
        ids = lax.broadcasted_iota(jnp.int32, (16, 8), 1).astype(F32)
        place = lax.broadcasted_iota(jnp.int32, (16, rows), 1)
        row = lax.broadcasted_iota(jnp.int32, (16, rows), 0)
        for h in range(2):
            mine = place == row + (ex * CAP + h * 16)
            slope_col = jnp.sum(jnp.where(mine, slope[2, 0:1, :], 0.0), axis=1, keepdims=True)
            inner_col = jnp.sum(jnp.where(mine, slope[2, 4:5, :], 0.0), axis=1, keepdims=True)
            weight, inv = col(1, h, 0), col(1, h, 1)
            cot = slope_col * col(1, h, 2)
            both = jnp.where(ids == col(1, h, 3), 1.0, 0.0) - jnp.where(ids == col(1, h, 4), 1.0, 0.0)
            dlog = cot * both
            dn = weight * summed(m, h)
            for e in range(8):
                dn = dn + dlog[:, e:e + 1] * router_c[e:e + 1, :]
            coef = inv * inv * (weight * inner_col + cot * col(1, h, 5)) / depth
            change = inv * (dn * gain_c) - coef * xb[c, h].astype(F32)
            xb[c, h] = (gath[c, y, z, h].astype(F32) + change).astype(BF16)
        row_b_msg(c)[0]()

    def halves(value):
        return value.reshape(2, 16, width)

    def pick(onehot, k, c):
        source_copy(k, c).wait()
        return jnp.dot(onehot, source[:, span(c)], preferred_element_type=F32)

    def select(k, onehot, named):
        tok = named.shape[1]
        eye = lax.broadcasted_iota(jnp.int32, (tok, tok), 0) == lax.broadcasted_iota(jnp.int32, (tok, tok), 1)
        sel[k, 0:tok, :] = jnp.where(eye, 1.0 - named, 0.0).astype(BF16)
        sel[k, tok:tok + CAP, :] = onehot

    def onehot_of(k):
        return sel[k, sel.shape[2]:sel.shape[2] + CAP, :]

    def route(k, array, kept):
        onehot = onehot_of(k)
        total = jnp.zeros((CAP, 1), F32)
        for c in range(NC):
            x = pick(onehot, array, c)
            kept[c] = halves(x.astype(BF16))
            total = total + jnp.sum(x * x, axis=1, keepdims=True)
        inverse = lax.rsqrt(total / depth + EPS)
        logits = jnp.zeros((CAP, 8), F32)
        for c in range(NC):
            normed = kept[c].reshape(CAP, width).astype(F32) * inverse * gain[:, span(c)]
            gath[array * NC + c, y, z] = halves(normed.astype(BF16))
            logits = logits + lax.dot_general(
                normed, router_t[:, span(c)], LAST, precision=HI, preferred_element_type=F32
            )
        wide = jnp.concatenate([routes[k].astype(F32), jnp.zeros((6, routes.shape[2]), F32)], axis=0)
        experts = lax.dot_general(onehot, wide.astype(BF16), LAST, preferred_element_type=F32)
        first, second = experts[:, 0:1], experts[:, 1:2]
        ids = lax.broadcasted_iota(jnp.int32, (CAP, 8), 1).astype(F32)
        picked1 = jnp.sum(jnp.where(ids == first, logits, 0.0), axis=1, keepdims=True)
        picked2 = jnp.sum(jnp.where(ids == second, logits, 0.0), axis=1, keepdims=True)
        share = jax.nn.sigmoid(picked1 - picked2)
        on1 = jnp.where(first == 0.0, 1.0, 0.0)
        on2 = jnp.where(second == 0.0, 1.0, 0.0)
        weight = share * on1 + (1.0 - share) * on2
        if k == 1:
            weight = weight.astype(BF16).astype(F32)
        table = jnp.zeros((CAP, 128), F32)
        lane = lax.broadcasted_iota(jnp.int32, (CAP, 128), 1)
        for j, value in enumerate(
            (weight, inverse, (on1 - on2) * share * (1.0 - share), first, second, picked1 - picked2)
        ):
            table = jnp.where(lane == j, value, table)
        stats[k] = table

    small[0].wait()
    onehot_b, named_b = chosen(routes[1])
    pl.semaphore_wait(barrier, 6)
    for c in range(NC):
        gath[c, y, z] = halves(pick(onehot_b, 0, c).astype(BF16))
        start_all(one(0, c))
        source_copy(1, c).start()
    select(1, onehot_b, named_b)
    start_all(pass_msgs((0, 1)))
    for k in (1, 2, 3):
        small[k].wait()
    select(0, *chosen(routes[0]))
    route(0, 1, xf)
    for c in range(NC):
        source_copy(2, c).start()
    for c in range(NC):
        weight_copies(c)[0].start()
    for c in range(NC):
        weight_copies(c)[1].start()
        weight_copies(c)[2].start()
    gacc[...] = jnp.zeros_like(gacc)
    uacc[...] = jnp.zeros_like(uacc)
    bacc[...] = jnp.zeros_like(bacc)

    def when_in(value, low, high):
        return pl.when(jnp.logical_and(value >= low, value < high))

    slope_at = n_ag + 1 + 2 * LAG

    def step(t, _):
        @when_in(t, 0, NC)
        def _():
            finish_all(one(0, t))
            start_all(one(1, t))

        @when_in(t, 1, NC + 1)
        def _():
            finish_all(one(1, t - 1))

        for k, (go, relay, end) in ((1, (1, 3, NC)), (2, (NC, NC + 2, 2 * NC - 1))):
            @pl.when(t == relay)
            def _():
                finish_all(group(0, k))
                start_all(group(1, k))

            @pl.when(t == end)
            def _():
                finish_all(group(1, k))

        @when_in(t, 1, n_ag + 1)
        def _():
            start_all(ag3(t - 1))

        n = t - 1 - LAG

        @when_in(n, 0, n_ag)
        def _():
            finish_all(ag3(n))
            start_all(ag4(n))

        n = t - 1 - 2 * LAG

        @when_in(n, 0, n_ag)
        def _():
            finish_all(ag4(n))

        @pl.when(t == 1)
        def _():
            start_all(group(0, 1))

        @pl.when(t == NC)
        def _():
            start_all(group(0, 2))

        r = t - t_rs

        @when_in(r, 0, n_rs)
        def _():
            start_all(rs1(r))

        m1, m2, m3, m4 = (r - k * LAG for k in (1, 2, 3, 4))

        @when_in(m1, 0, n_rs)
        def _():
            finish_all(rs1(m1))
            add1(m1)
            start_all(rs2(m1))

        @when_in(m2, 0, n_rs)
        def _():
            finish_all(rs2(m2))
            add2(m2)
            start_all(rs3(m2))

        @when_in(m3, 0, n_rs)
        def _():
            finish_all(rs3(m3))
            add3(m3)
            start_all(rs4(m3))

        @when_in(m4, 0, n_rs)
        def _():
            finish_all(rs4(m4))

        @when_in(m4, 0, NC)
        def _():
            finish_forward(m4)

        @pl.when(m4 == NC - 1)
        def _():
            row_f_msg[0]()

        @pl.when(t == slope_at + 0)
        def _():
            start_all(sl_msgs(0, 0))

        @pl.when(t == slope_at + 1)
        def _():
            finish_all(sl_msgs(0, 0))
            start_all(sl_msgs(0, 1))

        @pl.when(t == slope_at + 2)
        def _():
            finish_all(sl_msgs(0, 1))
            sl_sum(0)
            start_all(sl_msgs(1, 0))

        @pl.when(t == slope_at + 3)
        def _():
            finish_all(sl_msgs(1, 0))
            start_all(sl_msgs(1, 1))

        @pl.when(t == slope_at + 4)
        def _():
            finish_all(sl_msgs(1, 1))
            sl_sum(1)

        @when_in(m4, NC, n_rs)
        def _():
            finish_backward(m4)

        @when_in(n, 0, NC)
        def _():
            weight_copies(n)[0].wait()
            bacc[...] += lax.dot_general(lhs(n), dw[n], LAST, preferred_element_type=F32)

        @when_in(n, NC, 2 * NC)
        def _():
            weight_copies(n - NC)[1].wait()
            weight_copies(n - NC)[2].wait()

        @when_in(n, NC, n_ag)
        def _():
            c = n % NC
            gacc[...] += jnp.dot(lhs(n), gw[c], preferred_element_type=F32)
            uacc[...] += jnp.dot(lhs(n), uw[c], preferred_element_type=F32)

        @pl.when(t == NC - 2)
        def _():
            route(1, 2, xb)
            start_all(pass_msgs((2, 3)))

        @pl.when(n == 2 * NC - 1)
        def _():
            lax.fori_loop(0, rows // 64, fwd_rows, 0)

        @pl.when(n == n_ag - 1)
        def _():
            lax.fori_loop(0, rows // 128, bwd_rows, 0)

        m = r + 1
        shape = part.shape[1:]

        @when_in(m, 0, NC)
        def _():
            part[m % NS] = jnp.dot(activ[...], dw[m], preferred_element_type=F32).astype(BF16).reshape(shape)

        @when_in(m, NC, n_rs)
        def _():
            c = m - NC
            value = lax.dot_general(gcot[...], gw[c], LAST, preferred_element_type=F32)
            value = value + lax.dot_general(ucot[...], uw[c], LAST, preferred_element_type=F32)
            part[m % NS] = value.astype(BF16).reshape(shape)

        return 0

    lax.fori_loop(0, t_rs + n_rs + 4 * LAG, step, 0)

    finish_all(pass_msgs((0, 1, 2, 3)))
    row_f_msg[1]()

    def drain(c, _):
        row_b_msg(c)[1]()
        return 0

    lax.fori_loop(0, NC, drain, 0)


def merge_kernel(sel_f, sel_b, act, grad, rows_f, rows_b, out_f, out_b):
    width = rows_f.shape[-1]
    tok = act.shape[0]
    first = (((0,), (0,)), ((), ()))
    for sel, plain, rows, out in ((sel_f, act, rows_f, out_f), (sel_b, grad, rows_b, out_b)):
        for c in range(rows.shape[0]):
            at = slice(c * width, (c + 1) * width)
            moved = lax.dot_general(
                sel[tok:tok + CAP, :], rows[c].reshape(CAP, width), first, preferred_element_type=F32
            )
            stay = lax.dot_general(sel[0:tok, :], plain[:, at], first, preferred_element_type=F32)
            out[:, at] = (moved + stay).astype(BF16)


def local(act_in, saved_in, grad_in, fwd_routes, bwd_routes, w_gate, w_up, w_down, router, norm_gain):
    act, saved, grad = act_in[0], saved_in[0], grad_in[0]
    rt_f, rt_b = fwd_routes[0].T, bwd_routes[0].T
    router_t = router[0].T
    tok, depth = act.shape
    width = depth // NC
    hid = w_gate.shape[2]
    rows = 16 * CAP
    sds = jax.ShapeDtypeStruct
    anywhere = pl.BlockSpec(memory_space=pl.ANY)
    dma = pltpu.SemaphoreType.DMA
    row_shape = (NC, 2, 16, width)
    sel_shape = (tok + CAP, tok)

    V = pltpu.VMEM
    rows_f, rows_b, sel_f, sel_b, act2, grad2 = pl.pallas_call(
        main_kernel,
        out_shape=(
            sds(row_shape, BF16), sds(row_shape, BF16),
            sds(sel_shape, BF16), sds(sel_shape, BF16),
            sds(act.shape, BF16), sds(grad.shape, BF16),
        ),
        in_specs=[anywhere] * 10,
        out_specs=(anywhere,) * 6,
        scratch_shapes=[
            V((tok, depth), BF16), V((2, 2, tok), jnp.int32), V(router_t.shape, F32), V((1, depth), F32),
            V(row_shape, BF16), V(row_shape, BF16), V((2, CAP, 128), F32), V((2,) + sel_shape, BF16),
            V((3 * NC, 4, 4, 2, 16, width), BF16),
            V((NC, width, hid), BF16), V((NC, width, hid), BF16), V((NC, hid, width), BF16),
            V((rows, hid), F32), V((rows, hid), F32), V((rows, hid), F32),
            V((rows, hid), BF16), V((rows, hid), BF16), V((rows, hid), BF16),
            V((NS, 4, 4, 2, 16, width), BF16),
            V((2, 2, NS, 2, 16, width), BF16), V((2, 2, NS, 4, 16, width), BF16),
            V((2, NS, 4, 16, width), BF16),
            V((2, 2, NS, 16, width // 2), BF16), V((2, 2, NS, 16, width), BF16),
            V((3, 8, rows), F32), V((2, 3, 8, rows), F32),
            dma((2, 2, 2, NC)), dma((2, 2, 2, NC)),
            dma((2, 2, 2, 2)), dma((2, 2, 2, 2)),
            dma((2, 2, 2, NG)), dma((2, 2, 2, NG)),
            dma((4, 2, 2, NS)), dma((4, 2, 2, NS)),
            dma((2, 3)), dma((2, 3)),
            dma((6, NC)), dma((4,)), dma((4,)), dma((4,)), dma((NC + 1,)), dma((NC + 1,)),
        ],
        compiler_params=pltpu.CompilerParams(
            collective_id=0, has_side_effects=True, vmem_limit_bytes=67_043_328
        ),
    )(act, saved, grad, rt_f, rt_b, router_t, norm_gain, w_gate[0], w_up[0], w_down[0])

    whole = pl.BlockSpec(sel_shape, lambda c: (0, 0))
    columns = pl.BlockSpec((tok, depth // MERGE), lambda c: (0, c))
    slots = pl.BlockSpec((NC // MERGE, 2, 16, width), lambda c: (c, 0, 0, 0))
    out_f, out_b = pl.pallas_call(
        merge_kernel,
        grid=(MERGE,),
        out_shape=(sds(act.shape, BF16), sds(grad.shape, BF16)),
        in_specs=[whole, whole, columns, columns, slots, slots],
        out_specs=(columns, columns),
    )(sel_f, sel_b, act2, grad2, rows_f, rows_b)
    return (out_f[None], out_b[None])


def solution(mesh):
    in_specs = (
        P("section", "expert", None),
        P("section", "expert", None),
        P("section", "expert", None),
        P("section", "expert", None),
        P("section", "expert", None),
        P("section", None, "expert"),
        P("section", None, "expert"),
        P("section", "expert", None),
        P("section", None, None),
        P("section", None),
    )
    out_specs = (P("section", "expert", None), P("section", "expert", None))
    return jax.shard_map(local, mesh=mesh, in_specs=in_specs, out_specs=out_specs, check_vma=False)
```

time: 209 us -> 185 us (0.89)
  Pallas kernels: 198 us -> 185 us
  local copies, waits for them, and re-layouts: 10.3 us -> 0 us
    unnamed x22 -> x0, local copies, waits for them, and re-layouts: 10.3 us -> none
    pallas_call x1, Pallas kernels: 188 us -> 180 us  [local(): pl.pallas_call(main_kernel, out_shape=(sds(row_shape, BF16), sds(row_shap...]
    pallas_call x2 -> x1, Pallas kernels: 9.86 us -> 4.81 us  [local(): pl.pallas_call(merge_kernel, grid=(MERGE,), out_shape=(sds(act.shape, BF1...]
where the time goes in v2:
time: 185 us
  Pallas kernels  185 us (100%)
    pallas_call x1, Pallas kernels, local(): pl.pallas_call(main_kernel, out_shape=(sds(row_shape, BF16), sds(row_shap...  180 us
    pallas_call x1, Pallas kernels, local(): pl.pallas_call(merge_kernel, grid=(MERGE,), out_shape=(sds(act.shape, BF1...  4.81 us

profile of v2, /device:TPU:1, one launch (start us, length us, event | category | flops | bytes accessed | tf_op | source)
XLA Modules:
  0.0 185.3 jit_solution(8541278990982280282)
XLA Ops:
  0.6 179.9 %shard_map.113 = (bf16[4,2,16,1536]{3,2,1,0:T(8,128)(2,1)}, bf16[4,2,16,1536]{3,2,1,0:T(8,128)(2,1)}, bf16[160,128]{1,0:T(8,128)(2,1)}, bf16[160,128]{1,0:T(8,12...) custom-call(bf16[128,6144]{1,0:T(8,128)(2,1)} %bitcast.20, bf16[128,6144]{1,0:T(8,128)(2,1)} %bitcast.21, ...), custom_call_target="tpu_custom_call" | custom-call | tf_op jit(solution)/shard_map/pallas_call | solution.py:653
  180.5 4.8 %shard_map.114 = (bf16[128,6144]{1,0:T(8,128)(2,1)}, bf16[128,6144]{1,0:T(8,128)(2,1)}) custom-call(bf16[160,128]{1,0:T(8,128)(2,1)} %get-tuple-element.10.sel_f, bf16[160,128]{1,0:T(8,128)(2,1)} %get-tuple-element.11.sel_b, bf16[128,6144]{1,0:T(8,128)(2,1)} %get-tuple-element.12.act, bf16[128,6144]{1,0:T(8,128)(2,1)} %get-tuple-element.13.grad, ...), custom_call_target="tpu_custom_call" | custom-call | tf_op jit(solution)/shard_map/pallas_call | solution.py:689

commit v3 on v2

--- a/solution.py
+++ b/solution.py
@@ -199,10 +199,10 @@
     def p_idx(slot, fa, sa, h):
         return (slot, sa, fa, h) if h == 0 else (slot, fa, sa, h)
 
-    def rs1(m):
+    def rs1(m, hs=(0, 1)):
         out = []
         slot = m % NS
-        for h in range(2):
+        for h in hs:
             f, s, first, _ = rs_pos(h)
             for i, d in enumerate(DIRS):
                 into = r1.at[h, i, slot]
@@ -210,10 +210,10 @@
                                rs_s.at[0, h, i, slot], rs_r.at[0, h, i, slot], first(d)))
         return out
 
-    def rs2(m):
+    def rs2(m, hs=(0, 1)):
         out = []
         slot = m % NS
-        for h in range(2):
+        for h in hs:
             f, s, first, _ = rs_pos(h)
             for i, d in enumerate(DIRS):
                 into = r2.at[h, i, slot]
@@ -221,10 +221,10 @@
                                rs_s.at[1, h, i, slot], rs_r.at[1, h, i, slot], first(d)))
         return out
 
-    def rs3(m):
+    def rs3(m, hs=(0, 1)):
         out = []
         slot = m % NS
-        for h in range(2):
+        for h in hs:
             f, s, _, second = rs_pos(h)
             for i, d in enumerate(DIRS):
                 into = r3.at[h, i, slot]
@@ -232,10 +232,10 @@
                                rs_s.at[2, h, i, slot], rs_r.at[2, h, i, slot], second(d)))
         return out
 
-    def rs4(m):
+    def rs4(m, hs=(0, 1)):
         out = []
         slot = m % NS
-        for h in range(2):
+        for h in hs:
             f, s, _, second = rs_pos(h)
             for i, d in enumerate(DIRS):
                 into = r4.at[h, i, slot]
@@ -243,24 +243,24 @@
                                rs_s.at[3, h, i, slot], rs_r.at[3, h, i, slot], second(d)))
         return out
 
-    def add1(m):
+    def add1(m, hs):
         slot = m % NS
-        for h in range(2):
+        for h in hs:
             f = rs_pos(h)[0]
             for i, d in enumerate(DIRS):
                 at = p_idx(slot, turn(f, d), PAIR[i], h)
                 part[at] = (part[at].astype(F32) + r1[h, i, slot].astype(F32)).astype(BF16)
 
-    def add2(m):
+    def add2(m, hs):
         slot = m % NS
-        for h in range(2):
+        for h in hs:
             f = rs_pos(h)[0]
             mine = part[p_idx(slot, f, ALL, h)].astype(F32)
             q[h, slot] = (mine + r2[h, 0, slot].astype(F32) + r2[h, 1, slot].astype(F32)).astype(BF16)
 
-    def add3(m):
+    def add3(m, hs):
         slot = m % NS
-        for h in range(2):
+        for h in hs:
             s = rs_pos(h)[1]
             for i, d in enumerate(DIRS):
                 to = turn(s, d)
@@ -432,17 +432,6 @@
         source_copy(1, c).start()
     select(1, onehot_b, named_b)
     start_all(pass_msgs((0, 1)))
-    for k in (1, 2, 3):
-        small[k].wait()
-    select(0, *chosen(routes[0]))
-    route(0, 1, xf)
-    for c in range(NC):
-        source_copy(2, c).start()
-    for c in range(NC):
-        weight_copies(c)[0].start()
-    for c in range(NC):
-        weight_copies(c)[1].start()
-        weight_copies(c)[2].start()
     gacc[...] = jnp.zeros_like(gacc)
     uacc[...] = jnp.zeros_like(uacc)
     bacc[...] = jnp.zeros_like(bacc)
@@ -491,7 +480,18 @@
 
         @pl.when(t == 1)
         def _():
+            for k in (1, 2, 3):
+                small[k].wait()
+            select(0, *chosen(routes[0]))
+            route(0, 1, xf)
             start_all(group(0, 1))
+            for c in range(NC):
+                source_copy(2, c).start()
+            for c in range(NC):
+                weight_copies(c)[0].start()
+            for c in range(NC):
+                weight_copies(c)[1].start()
+                weight_copies(c)[2].start()
 
         @pl.when(t == NC)
         def _():
@@ -507,21 +507,24 @@
 
         @when_in(m1, 0, n_rs)
         def _():
-            finish_all(rs1(m1))
-            add1(m1)
-            start_all(rs2(m1))
+            for h in range(2):
+                finish_all(rs1(m1, (h,)))
+                add1(m1, (h,))
+                start_all(rs2(m1, (h,)))
 
         @when_in(m2, 0, n_rs)
         def _():
-            finish_all(rs2(m2))
-            add2(m2)
-            start_all(rs3(m2))
+            for h in range(2):
+                finish_all(rs2(m2, (h,)))
+                add2(m2, (h,))
+                start_all(rs3(m2, (h,)))
 
         @when_in(m3, 0, n_rs)
         def _():
-            finish_all(rs3(m3))
-            add3(m3)
-            start_all(rs4(m3))
+            for h in range(2):
+                finish_all(rs3(m3, (h,)))
+                add3(m3, (h,))
+                start_all(rs4(m3, (h,)))
 
         @when_in(m4, 0, n_rs)
         def _():
@@ -580,7 +583,7 @@
             gacc[...] += jnp.dot(lhs(n), gw[c], preferred_element_type=F32)
             uacc[...] += jnp.dot(lhs(n), uw[c], preferred_element_type=F32)
 
-        @pl.when(t == NC - 2)
+        @pl.when(t == NC - 1)
         def _():
             route(1, 2, xb)
             start_all(pass_msgs((2, 3)))
@@ -623,16 +626,12 @@
 
 def merge_kernel(sel_f, sel_b, act, grad, rows_f, rows_b, out_f, out_b):
     width = rows_f.shape[-1]
-    tok = act.shape[0]
     first = (((0,), (0,)), ((), ()))
     for sel, plain, rows, out in ((sel_f, act, rows_f, out_f), (sel_b, grad, rows_b, out_b)):
         for c in range(rows.shape[0]):
             at = slice(c * width, (c + 1) * width)
-            moved = lax.dot_general(
-                sel[tok:tok + CAP, :], rows[c].reshape(CAP, width), first, preferred_element_type=F32
-            )
-            stay = lax.dot_general(sel[0:tok, :], plain[:, at], first, preferred_element_type=F32)
-            out[:, at] = (moved + stay).astype(BF16)
+            both = jnp.concatenate([plain[:, at], rows[c].reshape(CAP, width)], axis=0)
+            out[:, at] = lax.dot_general(sel[...], both, first, preferred_element_type=F32).astype(BF16)
 
 
 def local(act_in, saved_in, grad_in, fwd_routes, bwd_routes, w_gate, w_up, w_down, router, norm_gain):

time: 185 us -> 185 us (level)
  no operation moved by 1% of the time
where the time goes in v3:
time: 185 us; the launch traced here: 184 us
  Pallas kernels  184 us (99%)
    pallas_call x1, Pallas kernels, local(): pl.pallas_call(main_kernel, out_shape=(sds(row_shape, BF16), sds(row_shap...  180 us
    pallas_call x1, Pallas kernels, local(): pl.pallas_call(merge_kernel, grid=(MERGE,), out_shape=(sds(act.shape, BF1...  4.06 us

profile of v3, /device:TPU:1, one launch (start us, length us, event | category | flops | bytes accessed | tf_op | source)
XLA Modules:
  0.0 184.5 jit_solution(13236133937458113849)
XLA Ops:
  0.6 179.8 %shard_map.113 = (bf16[4,2,16,1536]{3,2,1,0:T(8,128)(2,1)}, bf16[4,2,16,1536]{3,2,1,0:T(8,128)(2,1)}, bf16[160,128]{1,0:T(8,128)(2,1)}, bf16[160,128]{1,0:T(8,12...) custom-call(bf16[128,6144]{1,0:T(8,128)(2,1)} %bitcast.20, bf16[128,6144]{1,0:T(8,128)(2,1)} %bitcast.21, ...), custom_call_target="tpu_custom_call" | custom-call | tf_op jit(solution)/shard_map/pallas_call | solution.py:652
  180.4 4.1 %shard_map.114 = (bf16[128,6144]{1,0:T(8,128)(2,1)}, bf16[128,6144]{1,0:T(8,128)(2,1)}) custom-call(bf16[160,128]{1,0:T(8,128)(2,1)} %get-tuple-element.10.sel_f, bf16[160,128]{1,0:T(8,128)(2,1)} %get-tuple-element.11.sel_b, bf16[128,6144]{1,0:T(8,128)(2,1)} %get-tuple-element.12.act, bf16[128,6144]{1,0:T(8,128)(2,1)} %get-tuple-element.13.grad, ...), custom_call_target="tpu_custom_call" | custom-call | tf_op jit(solution)/shard_map/pallas_call | solution.py:688

commit v4 on v3

--- a/solution.py
+++ b/solution.py
@@ -11,8 +11,9 @@
 NC = 4
 MERGE = 2
 CAP = 32
-LAG = 2
-NS = 2 * LAG + 1
+LAG = 1
+LAG_R = 2
+NS = 2 * LAG_R + 1
 NG = 8
 F32 = jnp.float32
 BF16 = jnp.bfloat16
@@ -37,7 +38,7 @@
     rows_f, rows_b, sel_f, sel_b, act2, grad2,
     source, routes, router_t, gain, xf, xb, stats, sel,
     gath, gw, uw, dw, gacc, uacc, bacc, activ, gcot, ucot,
-    part, r1, r2, q, r3, r4, slope, slope_in,
+    part, r1, r2, q, r3, r4, ready, slope, slope_in,
     one_s, one_r, grp_s, grp_r, ag_s, ag_r, rs_s, rs_r, sl_s, sl_r,
     in_sem, small_sem, pass_s, pass_r, row_s, row_r,
 ):
@@ -47,7 +48,7 @@
     rows = gacc.shape[0]
     depth = gain.shape[1]
     n_ag, n_rs = 3 * NC, 2 * NC
-    t_rs = n_ag + 1
+    t_rs = n_ag - 1
     n_sec = lax.axis_size("section")
 
     sec = lax.axis_index("section")
@@ -348,8 +349,7 @@
         for h in range(2):
             xf[m, h] = (xf[m, h].astype(F32) + col(0, h, 0) * summed(m, h)).astype(BF16)
 
-    def finish_backward(m):
-        c = m - NC
+    def prepare_backward(c):
         at = pl.ds(pl.multiple_of(c * width, 128), width)
         router_c = router_t[:, at]
         gain_c = gain[:, at]
@@ -364,12 +364,19 @@
             cot = slope_col * col(1, h, 2)
             both = jnp.where(ids == col(1, h, 3), 1.0, 0.0) - jnp.where(ids == col(1, h, 4), 1.0, 0.0)
             dlog = cot * both
-            dn = weight * summed(m, h)
-            for e in range(8):
+            dn = dlog[:, 0:1] * router_c[0:1, :]
+            for e in range(1, 8):
                 dn = dn + dlog[:, e:e + 1] * router_c[e:e + 1, :]
             coef = inv * inv * (weight * inner_col + cot * col(1, h, 5)) / depth
             change = inv * (dn * gain_c) - coef * xb[c, h].astype(F32)
-            xb[c, h] = (gath[c, y, z, h].astype(F32) + change).astype(BF16)
+            ready[c, h] = gath[c, y, z, h].astype(F32) + change
+
+    def finish_backward(m):
+        c = m - NC
+        gain_c = gain[:, pl.ds(pl.multiple_of(c * width, 128), width)]
+        for h in range(2):
+            scale = col(1, h, 0) * col(1, h, 1)
+            xb[c, h] = (ready[c, h] + scale * (summed(m, h) * gain_c)).astype(BF16)
         row_b_msg(c)[0]()
 
     def halves(value):
@@ -503,7 +510,7 @@
         def _():
             start_all(rs1(r))
 
-        m1, m2, m3, m4 = (r - k * LAG for k in (1, 2, 3, 4))
+        m1, m2, m3, m4 = (r - k * LAG_R for k in (1, 2, 3, 4))
 
         @when_in(m1, 0, n_rs)
         def _():
@@ -567,6 +574,12 @@
         def _():
             finish_backward(m4)
 
+        early = t - (slope_at + 5)
+
+        @when_in(early, 0, NC)
+        def _():
+            prepare_backward(early)
+
         @when_in(n, 0, NC)
         def _():
             weight_copies(n)[0].wait()
@@ -612,7 +625,7 @@
 
         return 0
 
-    lax.fori_loop(0, t_rs + n_rs + 4 * LAG, step, 0)
+    lax.fori_loop(0, t_rs + n_rs + 4 * LAG_R, step, 0)
 
     finish_all(pass_msgs((0, 1, 2, 3)))
     row_f_msg[1]()
@@ -669,7 +682,7 @@
             V((2, 2, NS, 2, 16, width), BF16), V((2, 2, NS, 4, 16, width), BF16),
             V((2, NS, 4, 16, width), BF16),
             V((2, 2, NS, 16, width // 2), BF16), V((2, 2, NS, 16, width), BF16),
-            V((3, 8, rows), F32), V((2, 3, 8, rows), F32),
+            V(row_shape, F32), V((3, 8, rows), F32), V((2, 3, 8, rows), F32),
             dma((2, 2, 2, NC)), dma((2, 2, 2, NC)),
             dma((2, 2, 2, 2)), dma((2, 2, 2, 2)),
             dma((2, 2, 2, NG)), dma((2, 2, 2, NG)),

time: 185 us -> 184 us (level)
  no operation moved by 1% of the time
where the time goes in v4:
time: 184 us
  Pallas kernels  184 us (100%)
    pallas_call x1, Pallas kernels, local(): pl.pallas_call(main_kernel, out_shape=(sds(row_shape, BF16), sds(row_shap...  180 us
    pallas_call x1, Pallas kernels, local(): pl.pallas_call(merge_kernel, grid=(MERGE,), out_shape=(sds(act.shape, BF1...  4.05 us

profile of v4, /device:TPU:1, one launch (start us, length us, event | category | flops | bytes accessed | tf_op | source)
XLA Modules:
  0.0 184.2 jit_solution(8325181141750280984)
XLA Ops:
  0.6 179.5 %shard_map.113 = (bf16[4,2,16,1536]{3,2,1,0:T(8,128)(2,1)}, bf16[4,2,16,1536]{3,2,1,0:T(8,128)(2,1)}, bf16[160,128]{1,0:T(8,128)(2,1)}, bf16[160,128]{1,0:T(8,12...) custom-call(bf16[128,6144]{1,0:T(8,128)(2,1)} %bitcast.20, bf16[128,6144]{1,0:T(8,128)(2,1)} %bitcast.21, ...), custom_call_target="tpu_custom_call" | custom-call | tf_op jit(solution)/shard_map/pallas_call | solution.py:665
  180.1 4.1 %shard_map.114 = (bf16[128,6144]{1,0:T(8,128)(2,1)}, bf16[128,6144]{1,0:T(8,128)(2,1)}) custom-call(bf16[160,128]{1,0:T(8,128)(2,1)} %get-tuple-element.10.sel_f, bf16[160,128]{1,0:T(8,128)(2,1)} %get-tuple-element.11.sel_b, bf16[128,6144]{1,0:T(8,128)(2,1)} %get-tuple-element.12.act, bf16[128,6144]{1,0:T(8,128)(2,1)} %get-tuple-element.13.grad, ...), custom_call_target="tpu_custom_call" | custom-call | tf_op jit(solution)/shard_map/pallas_call | solution.py:701
